TPU v7x, 32 devices: a whole 2x2x4 slice. The times are simulated.
32 devices in a mesh: groups: 2 (over y), seq: 4 (over z), head: 4 (over x, core).
Axes of the slice: x: 2, y: 2, z: 4, core: 2. Of those that a mesh axis runs over, the one named last changes fastest.
Arguments:
- queries: bfloat16 [32, 3, 32, 128], P('groups', None, 'head'), parts along dimension 0, may hold values from -8 to 8
- new_kv: bfloat16 [4, 16, 3, 4, 128], P('groups', None, None, 'head'), parts along dimension 0, may hold values from -16 to 16
- res_kv: bfloat16 [4, 2, 16384, 4, 128], P('groups', None, 'seq', 'head'), parts along dimension 0, may hold values from -16 to 16
- prefill_kv: bfloat16 [4, 4, 4096, 128], P('groups', None, ('seq', 'head')), parts along dimension 0, may hold values from -16 to 16
- block_table: int32 [128], P('groups'), parts along dimension 0, may hold values from 0 to 63, as said below
- lengths: int32 [6], P('groups'), parts along dimension 0, may hold values from 4096 to 16384, as said below
- join_step: int32 [2], P('groups'), parts along dimension 0, may hold values from 1 to 15
Outputs:
- attn_out: bfloat16 [32, 3, 32, 128], P('groups', None, 'head'), parts along dimension 0
- new_cache: bfloat16 [4, 4, 4096, 128], P('groups', 'head', 'seq'), parts along dimension 0
There are 2 independent parts, one for each index of `groups`. A program takes and returns all parts, laid end to end along the dimension named above; each array names one. Nothing has to cross between parts.
Inputs may be any that keep to these rules, and one draw needn't show every extreme that they name: `block_table`: A permutation of 0 to 63. In each aligned run of 4 entries (the blocks of one prefill device) every aligned range of 16 slots is named exactly 1 times. `lengths`: entries 0 to 1 lie between 4096 and 16384, and one of them equals 16384; entry 2 equals 4096.
All inputs are finite; a program needn't handle non-finite values.
Results may differ from a plain program's by a relative error of at most 0.0039.
Values may be sent and summed in bfloat16 or wider, within the bound.
No kernel may reach another device: no remote copies, remote signals or barrier semaphores. Data moves between devices by JAX's collectives and lax.ppermute only.
A program may use at most 64 MiB of HBM per device.

v0:
```python
import math

import jax
import jax.numpy as jnp
from jax import lax
from jax.sharding import PartitionSpec as P

very_low = -1e30


def merged_2(shard, axis, combine):
    everything = jax.tree.map(lambda part: lax.all_gather(part, axis), shard)
    initial = jax.tree.map(lambda part: part[0], everything)

    def lap(k, so_far):
        return combine(so_far, jax.tree.map(lambda part: part[k], everything))

    return lax.fori_loop(1, lax.axis_size(axis), lap, initial)


def partial_softmax(query_rows, key_rows, value_rows, valid_mask, score_scale):
    scores = (
        jnp.einsum("rd,pd->rp", query_rows, key_rows, preferred_element_type=jnp.float32)
        * score_scale
    )
    scores = jnp.where(valid_mask[None, :], scores, very_low)
    row_max = jnp.max(scores, axis=-1)
    weights = jnp.where(valid_mask[None, :], jnp.exp(scores - row_max[:, None]), 0.0)
    row_total = jnp.sum(weights, axis=-1)
    summed = jnp.einsum(
        "rp,pd->rd", weights.astype(jnp.bfloat16), value_rows, preferred_element_type=jnp.float32
    )
    return (row_max, row_total, summed)


def combine(earlier_part, later_part):
    joint_max = jnp.maximum(earlier_part[0], later_part[0])
    left_scale = jnp.exp(earlier_part[0] - joint_max)
    right_scale = jnp.exp(later_part[0] - joint_max)
    return (
        joint_max,
        earlier_part[1] * left_scale + later_part[1] * right_scale,
        earlier_part[2] * left_scale[..., None] + later_part[2] * right_scale[..., None],
    )


def per_device(queries, new_kv, res_kv, prefill_kv, block_table, lengths, join_step):
    seq_index = lax.axis_index("seq")
    head_index = lax.axis_index("head")
    seq_count = lax.axis_size("seq")
    head_count = lax.axis_size("head")
    senders = seq_count * head_count
    step_count, request_count, group_size, head_dim = queries.shape
    resident = res_kv.shape[1]
    res_rows = res_kv.shape[2]
    score_scale = 1.0 / math.sqrt(head_dim)
    joined = join_step[0]
    head_total = prefill_kv.shape[1]
    new_rows = prefill_kv.shape[2]
    total_blocks = block_table.shape[0]
    dev_blocks = total_blocks // senders
    block_len = new_rows // dev_blocks
    page_count = dev_blocks // seq_count
    slot_count = page_count * senders
    table_rows = block_table.reshape(senders, dev_blocks)
    sender = seq_index * head_count + head_index
    own_slots = lax.dynamic_slice_in_dim(table_rows, sender, 1, 0)[0]
    send_order = jnp.argsort(own_slots)
    blocks = prefill_kv.reshape(2, head_total, dev_blocks, block_len, head_dim)
    ordered = jnp.take(blocks, send_order, axis=2)
    sender_ids = jnp.arange(senders, dtype=jnp.int32)
    outgoing = jnp.swapaxes(ordered, 1, 2).reshape(2, senders, page_count * block_len, head_dim)
    arrived = lax.all_to_all(outgoing, ("seq", "head"), split_axis=1, concat_axis=1, tiled=True)
    inverse = (
        jnp.zeros((total_blocks,), jnp.int32)
        .at[block_table]
        .set(jnp.arange(total_blocks, dtype=jnp.int32))
    )
    rank_within = jnp.argsort(jnp.argsort(table_rows, axis=1), axis=1).reshape(-1)
    held_blocks = lax.dynamic_slice_in_dim(inverse, seq_index * slot_count, slot_count, 0)
    page_index = rank_within[held_blocks] - seq_index * page_count
    take_rows = sender_ids[held_blocks // dev_blocks] * page_count + page_index
    relaid = jnp.take(arrived, take_rows, axis=1)
    new_cache = relaid.reshape(2, 1, slot_count * block_len, head_dim)
    positions = (
        held_blocks[:, None] * block_len + jnp.arange(block_len, dtype=jnp.int32)[None, :]
    ).reshape(-1)
    partials = []
    res_positions = seq_index * res_rows + jnp.arange(res_rows, dtype=jnp.int32)
    for request in range(resident):
        query_rows = queries[:, request].reshape(step_count * group_size, head_dim)
        partials.append(
            partial_softmax(
                query_rows,
                res_kv[0, request, :, 0],
                res_kv[1, request, :, 0],
                res_positions < lengths[request],
                score_scale,
            )
        )
    query_rows = queries[:, resident].reshape(step_count * group_size, head_dim)
    partials.append(
        partial_softmax(
            query_rows, new_cache[0, 0], new_cache[1, 0], positions < lengths[resident], score_scale
        )
    )
    stacked_max = jnp.stack([member[0] for member in partials])
    stacked_total = jnp.stack([member[1] for member in partials])
    stacked_sum = jnp.stack([member[2] for member in partials])
    merged = merged_2((stacked_max, stacked_total, stacked_sum), "seq", combine)
    row_max = jnp.transpose(merged[0].reshape(request_count, step_count, group_size), (1, 0, 2))
    row_total = jnp.transpose(merged[1].reshape(request_count, step_count, group_size), (1, 0, 2))
    summed = jnp.transpose(
        merged[2].reshape(request_count, step_count, group_size, head_dim), (1, 0, 2, 3)
    )
    fresh_keys = new_kv[0, :, :, 0]
    fresh_values = new_kv[1, :, :, 0]
    fresh_scores = (
        jnp.einsum("trqd,urd->trqu", queries, fresh_keys, preferred_element_type=jnp.float32)
        * score_scale
    )
    step_ids = jnp.arange(step_count, dtype=jnp.int32)
    request_ids = jnp.arange(request_count, dtype=jnp.int32)
    allowed = (step_ids[None, None, :] <= step_ids[:, None, None]) & (
        (request_ids[None, :, None] < resident) | (step_ids[None, None, :] >= joined)
    )
    fresh_scores = jnp.where(allowed[:, :, None, :], fresh_scores, very_low)
    joint_max = jnp.maximum(row_max, jnp.max(fresh_scores, axis=-1))
    rescale = jnp.exp(row_max - joint_max)
    fresh_weight = jnp.where(
        allowed[:, :, None, :], jnp.exp(fresh_scores - joint_max[..., None]), 0.0
    )
    row_total = row_total * rescale + jnp.sum(fresh_weight, axis=-1)
    summed = summed * rescale[..., None] + jnp.einsum(
        "trqu,urd->trqd",
        fresh_weight.astype(jnp.bfloat16),
        fresh_values,
        preferred_element_type=jnp.float32,
    )
    result = summed / row_total[..., None]
    live_rows = (request_ids[None, :] < resident) | (step_ids[:, None] >= joined)
    attn_out = jnp.where(live_rows[:, :, None, None], result, 0.0).astype(jnp.bfloat16)
    return (attn_out, new_cache)


def solution(mesh):
    in_specs = (
        P("groups", None, "head", None),
        P("groups", None, None, "head", None),
        P("groups", None, "seq", "head", None),
        P("groups", None, ("seq", "head"), None),
        P("groups"),
        P("groups"),
        P("groups"),
    )
    out_specs = (P("groups", None, "head", None), P("groups", "head", "seq", None))
    return jax.shard_map(
        per_device, mesh=mesh, in_specs=in_specs, out_specs=out_specs, check_vma=False
    )
```

profile of v0, /device:TPU:0, one launch (start us, length us, event | category | flops | bytes accessed | tf_op | source)
XLA Modules:
  0.0 72.9 jit_solution(4330611319050637501)
XLA Ops:
  0.7 0.8 %reshape.206 = s32[16,4]{1,0:T(8,128)S(1)} reshape(s32[64]{0:T(128)} %param.13) | data formatting | bytes 512 | tf_op jit(solution)/shard_map/reshape | solution.py:65
  1.5 0.7 %sort.50 = (s32[4]{0:T(128)}, s32[4]{0:T(128)S(1)}) sort(s32[4]{0:T(128)S(1)} %dynamic-slice_bitcast_fusion, s32[4]{0:T(128)S(1)} %iota.68), dimensions={0}, to_apply=%region_5.6 | sort | flops 8 | bytes 64 | tf_op jit(solution)/shard_map/jit(argsort)/sort | solution.py:68
  2.3 0.6 gather_fusion.2
  2.9 0.1 select_bitcast_fusion
  3.1 0.8 %copy.40 = bf16[2,16,64,128]{3,2,0,1:T(8,128)(2,1)} copy(bf16[2,16,64,128]{3,2,1,0:T(8,128)(2,1)S(1)} %bitcast.150) | data formatting | bytes 1048576 | tf_op jit(solution)/shard_map/reshape | solution.py:72
  3.9 7.4 %all-to-all-start = ((bf16[2,16,64,128]{3,2,0,1:T(8,128)(2,1)}), bf16[2,16,64,128]{3,2,0,1:T(8,128)(2,1)S(1)}, u32[]{:S(2)}, u32[]{:S(2)}) async-start(bf16[2,16,64,128]{3,2,0,1:T(8,128)(2,1)} %copy.40), calls=%async_computation | async-start | bytes 1048576 | tf_op jit(solution)/shard_map/all_to_all | solution.py:73
  11.4 0.1 copy.37
  11.5 0.6 sort.48
  12.1 0.6 sort.49
  12.7 0.1 copy.38
  12.8 0.1 reshape.207
  12.9 0.8 %scatter_custom_fusion = s32[64]{0:T(128)S(1)} fusion(s32[64]{0:T(128)S(1)} %compare_select_fusion.4, s32[64]{0:T(128)S(1)} %iota.64, s32[]{:T(128)} %constant.95.clone.1), kind=kCustom, calls=%fused_computation.112 | custom fusion | bytes 260 | tf_op jit(solution)/shard_map/scatter | solution.py:77
  13.7 0.1 broadcast_multiply_fusion
  13.8 0.7 gather_fusion.1
  14.4 0.7 gather_fusion
  15.8 0.6 fusion.60
  16.4 0.6 add_compare_fusion
  17.1 0.1 lt.109
  17.2 0.1 broadcast_in_dim.168
  17.3 1.3 %fusion.47 = (pred[4096]{0:T(1024)(128)(4,1)S(1)}, pred[4096]{0:T(1024)(128)(4,1)S(1)}) fusion(s32[]{:T(128)} %bitcast.8, s32[]{:T(128)S(6)} %mul.118, s32[]{:T(128)} %bitcast.4), kind=kLoop, calls=%fused_computation.72 | loop fusion | flops 12288 | bytes 8204 | tf_op jit(solution)/shard_map/lt | solution.py:97
  18.6 1.7 %fusion.63 = (f32[128]{0:T(128)S(1)}, f32[128,4096]{1,0:T(8,128)S(1)}) fusion(bf16[2,2,4096,1,128]{4,2,3,1,0:T(8,128)(2,1)} %param.11, bf16[16,3,8,128]{3,2,1,0:T(8,128)(2,1)S(1)} %copy-done.2, pred[4096]{0:T(1024)(128)(4,1)S(1)} %get-tuple-element.237), kind=kOutput, calls=%fused_computation.121 | convolution fusion | flops 135790464 | bytes 3183104 | tf_op jit(solution)/shard_map/rd,pd->rp/dot_general | solution.py:23
  20.4 1.8 %fusion.64 = (f32[128]{0:T(128)S(1)}, f32[128,4096]{1,0:T(8,128)S(1)}) fusion(bf16[2,2,4096,1,128]{4,2,3,1,0:T(8,128)(2,1)} %param.11, bf16[16,3,8,128]{3,2,1,0:T(8,128)(2,1)S(1)} %copy-done.2, pred[4096]{0:T(1024)(128)(4,1)S(1)} %get-tuple-element.238), kind=kOutput, calls=%fused_computation.122 | convolution fusion | flops 135790464 | bytes 3183104 | tf_op jit(solution)/shard_map/rd,pd->rp/dot_general | solution.py:23
  22.2 0.1 broadcast_and_fusion
  22.3 0.5 fusion.8
  22.8 0.5 fusion.6
  23.4 0.4 fusion.61
  23.8 0.7 copy-done.1
  24.5 0.5 convolution_bitcast_fusion.1
  25.0 0.5 convolution_bitcast_fusion.2
  25.6 0.6 gather_fusion.3
  26.3 0.1 broadcast_select_fusion
  26.5 0.3 fusion.62
  26.8 0.2 fusion.32
  27.0 0.5 convolution_bitcast_fusion.3
  27.5 12.4 %all-gather.3 = f32[4,3,128]{2,1,0:T(4,128)S(1)} all-gather(f32[1,3,128]{2,1,0:T(4,128)S(1)} %maximum_bitcast_fusion), channel_id=2, replica_groups=mesh['groups'=2,'seq'=4,'head'=4] {'seq'}, dimensions={0}, use_global_device_ids=true | all-gather | bytes 7680 | tf_op jit(solution)/shard_map/all_gather | solution.py:12
  39.9 11.9 %all-gather.4 = f32[4,3,128]{2,1,0:T(4,128)S(1)} all-gather(f32[1,3,128]{2,1,0:T(4,128)S(1)} %maximum_bitcast_fusion.1), channel_id=3, replica_groups=mesh['groups'=2,'seq'=4,'head'=4] {'seq'}, dimensions={0}, use_global_device_ids=true | all-gather | bytes 7680 | tf_op jit(solution)/shard_map/all_gather | solution.py:12
  51.9 17.6 %all-gather.2 = f32[12,128,128]{2,1,0:T(8,128)S(1)} all-gather(f32[3,128,128]{2,1,0:T(8,128)S(1)} %pad_maximum_fusion), channel_id=4, replica_groups=mesh['groups'=2,'seq'=4,'head'=4] {'seq'}, dimensions={0}, use_global_device_ids=true | all-gather | bytes 983040 | tf_op jit(solution)/shard_map/all_gather | solution.py:12
  69.5 0.8 %while.19 = (s32[]{:T(128)}, f32[3,128]{1,0:T(4,128)S(1)}, f32[3,128]{1,0:T(4,128)S(1)}, f32[3,128,128]{2,1,0:T(8,128)S(1)}, f32[4,3,128]{2,1,0:T(4,128)S(1)}, /...) while((s32[]{:T(128)}, f32[3,128]{1,0:T(4,128)S(1)}, ...), condition=%wide.region_11.12_spmd, body=%wide.region_10.11_spmd.sunk | while | flops 149765 | bytes 605327 | solution.py:18
  69.5 0.2 fusion.71
  69.8 0.2 fusion.71
  70.0 0.2 fusion.71
  70.3 0.1 reshape.211
  70.4 0.1 reshape.212
  70.6 0.1 fusion.38
  70.9 0.1 copy.47
  71.0 0.2 fusion.15
  71.2 0.7 copy.51
  71.9 1.0 %bitcast_select_fusion = bf16[2,1,1024,128]{3,2,0,1:T(8,128)(2,1)} fusion(bf16[2,16,64,128]{3,2,1,0:T(8,128)(2,1)S(1)} %copy.50, pred[1024]{0:T(1024)(128)(4,1)S(1)} %broadcast_in_dim.168), kind=kLoop, calls=%fused_computation.50 | loop fusion | flops 262144 | bytes 1049600 | tf_op jit(solution)/shard_map/jit(_take)/select_n | solution.py:83
  (51 shorter events, 1.0 us)
Async XLA Ops:
  0.6 1.6 %copy-start = (bf16[2,4,256,128]{3,2,1,0:T(8,128)(2,1)S(1)}, bf16[2,4,256,128]{3,2,1,0:T(8,128)(2,1)}, u32[]{:S(2)}) copy-start(bf16[2,4,256,128]{3,2,1,0:T(8,128)(2,1)} %param.12) | copy-start | bytes 1572868
  2.9 8.4 %copy-start.5 = (s32[64]{0:T(128)S(1)}, s32[64]{0:T(128)}, u32[]{:S(2)}) copy-start(s32[64]{0:T(128)} %param.13) | copy-start | bytes 772
  3.0 12.8 %copy-start.4 = (s32[3]{0:T(128)S(1)}, s32[3]{0:T(128)}, u32[]{:S(2)}) copy-start(s32[3]{0:T(128)} %param.14) | copy-start | bytes 40
  3.1 15.6 %copy-start.2 = (bf16[16,3,8,128]{3,2,1,0:T(8,128)(2,1)S(1)}, bf16[16,3,8,128]{3,2,1,0:T(8,128)(2,1)}, u32[]{:S(2)}) copy-start(bf16[16,3,8,128]{3,2,1,0:T(8,128)(2,1)} %param.9) | copy-start | bytes 294916
  3.9 21.7 %all-to-all-start = ((bf16[2,16,64,128]{3,2,0,1:T(8,128)(2,1)}), bf16[2,16,64,128]{3,2,0,1:T(8,128)(2,1)S(1)}, u32[]{:S(2)}, u32[]{:S(2)}) async-start(bf16[2,16,64,128]{3,2,0,1:T(8,128)(2,1)} %copy.40), calls=%async_computation | async-start | bytes 1048576 | tf_op jit(solution)/shard_map/all_to_all | solution.py:73
  22.3 1.2 %copy-start.3 = (bf16[2,16,3,1,128]{4,1,3,2,0:T(8,128)(2,1)S(1)}, bf16[2,16,3,1,128]{4,1,3,2,0:T(8,128)(2,1)}, u32[]{:S(2)}) copy-start(bf16[2,16,3,1,128]{4,1,3,2,0:T(8,128)(2,1)} %param.10) | copy-start | bytes 73732
  22.3 2.2 %copy-start.1 = (bf16[2,2,4096,1,128]{4,2,3,1,0:T(8,128)(2,1)S(1)}, bf16[2,2,4096,1,128]{4,2,3,1,0:T(8,128)(2,1)}, u32[]{:S(2)}) copy-start(bf16[2,2,4096,1,128]{4,2,3,1,0:T(8,128)(2,1)} %param.11) | copy-start | bytes 12582916
where the time goes:
time: 73.3 us; the launch traced here: 72.9 us
  blocking collectives  41.9 us (57%)
  local copies, waits for them, and re-layouts  8.28 us (11%)
  other arithmetic  7.65 us (10%)
  starting transfers between devices  7.39 us (10%)
  matrix products  5.95 us (8%)
  between operations  1.63 us (2%)
    all_gather x3, blocking collectives, merged_2(): everything = jax.tree.map(lambda part: lax.all_gather(part, axis), shard)  41.9 us
    all_to_all x1, starting transfers between devices, per_device(): lax.all_to_all(outgoing, ('seq', 'head'), split_axis=1, concat_axis=1, ti...  7.39 us
    dot_general x3, matrix products, partial_softmax(): jnp.einsum('rd,pd->rp', query_rows, key_rows, preferred_element_type=jnp....  3.83 us
    dot_general x3, matrix products, partial_softmax(): jnp.einsum('rp,pd->rd', weights.astype(jnp.bfloat16), value_rows, preferr...  1.52 us
  transfers between devices with their start and end apart: 1, of which 0 were waited for; matrix products, arithmetic and copies ran while one was open for 17% of the time, Pallas kernels for 0%

commit v1 on v0

v1 whole, which is shorter than its diff:
```python
import functools
import math

import jax
import jax.numpy as jnp
from jax import lax
from jax.experimental import pallas as pl
from jax.experimental.pallas import tpu as pltpu
from jax.sharding import PartitionSpec as P

FLOOR = -1e30
MASKED = -2e30
PIECES = 3
LOG2E = math.log2(math.e)


def vmem():
    return pl.BlockSpec(memory_space=pltpu.VMEM)


def smem():
    return pl.BlockSpec(memory_space=pltpu.SMEM)


def anywhere():
    return pl.BlockSpec(memory_space=pl.ANY)


def query_rows(q_ref, request):
    steps, _, group, depth = q_ref.shape
    wide = q_ref[:, request].astype(jnp.float32)
    return wide.reshape(steps * group, depth).astype(jnp.bfloat16)


def empty_state(rows, depth):
    return (
        jnp.full((rows, 1), FLOOR, jnp.float32),
        jnp.zeros((rows, 1), jnp.float32),
        jnp.zeros((rows, depth), jnp.float32),
    )


def absorb(state, query, keys, values, scale, bias):
    row_max, total, summed = state
    scores = lax.dot_general(
        query, keys, (((1,), (1,)), ((), ())), preferred_element_type=jnp.float32
    )
    scores = scores * scale
    if bias is not None:
        scores = scores + bias
    new_max = jnp.maximum(row_max, jnp.max(scores, axis=1, keepdims=True))
    fade = jnp.exp2(row_max - new_max)
    weight = jnp.exp2(scores - new_max)
    total = total * fade + jnp.sum(weight, axis=1, keepdims=True)
    summed = summed * fade + jnp.dot(
        weight.astype(jnp.bfloat16), values, preferred_element_type=jnp.float32
    )
    return new_max, total, summed


def fresh_bias(steps, group, request, resident, joined, owner):
    rows = steps * group
    row_step = lax.broadcasted_iota(jnp.int32, (rows, steps), 0) // group
    key_step = lax.broadcasted_iota(jnp.int32, (rows, steps), 1)
    allowed = (key_step <= row_step) & owner
    if request >= resident:
        allowed = allowed & (key_step >= joined)
    return jnp.where(allowed, 0.0, MASKED)


def unit(rows):
    return lax.broadcasted_iota(jnp.int32, (rows, rows), 0) == lax.broadcasted_iota(
        jnp.int32, (rows, rows), 1
    )


def to_row(column, diagonal):
    return jnp.sum(jnp.where(diagonal, column, 0.0), axis=0, keepdims=True)


def to_column(row, diagonal):
    return jnp.sum(jnp.where(diagonal, row, 0.0), axis=1, keepdims=True)


def split(row):
    parts = []
    rest = row
    for _ in range(PIECES):
        part = rest.astype(jnp.bfloat16).astype(jnp.float32)
        parts.append(part)
        rest = rest - part
    return parts


def finish(state, diagonal):
    row_max, total, summed = state
    safe = jnp.where(total > 0.0, total, 1.0)
    return summed / safe, to_row(row_max + jnp.log2(safe), diagonal)


def tail_rows(levels):
    parts = [part for level in levels for part in split(level)]
    width = parts[0].shape[1]
    count = -(-len(parts) // 16) * 16
    parts.append(jnp.zeros((count - len(parts), width), jnp.float32))
    return jnp.concatenate(parts, axis=0).astype(jnp.bfloat16)


def pack_kernel(slots, table_ref, place_ref, block_ref, send_ref):
    _, heads, dev_blocks, _, _ = block_ref.shape
    for block in range(dev_blocks):
        shard = table_ref[place_ref[0] * dev_blocks + block] // slots
        for head in range(heads):
            for part in range(2):
                send_ref[shard * heads + head, part] = block_ref[part, head, block]


def resident_kernel(
    scale, chunk, len_ref, place_ref, q_ref, fresh_ref, kv_hbm, out_ref, level_ref, kv_ref, sems
):
    resident, length = kv_hbm.shape[1], kv_hbm.shape[2]
    steps, _, group, depth = q_ref.shape
    rows = steps * group
    count = length // chunk

    def copy(request, index, part):
        window = pl.ds(index * chunk, chunk)
        return pltpu.make_async_copy(
            kv_hbm.at[part, request, window],
            kv_ref.at[part, request, window],
            sems.at[part, request, index],
        )

    for request in range(resident):
        for index in range(count):
            for part in range(2):
                copy(request, index, part).start()
    diagonal = unit(rows)
    seq_index = place_ref[1]
    owner = seq_index == 0
    for request in range(resident):
        query = query_rows(q_ref, request)
        state = absorb(
            empty_state(rows, depth),
            query,
            fresh_ref[0, request],
            fresh_ref[1, request],
            scale,
            fresh_bias(steps, group, request, resident, 0, owner),
        )
        for index in range(count):
            copy(request, index, 0).wait()
            copy(request, index, 1).wait()
            start = seq_index * length + index * chunk
            position = start + lax.broadcasted_iota(jnp.int32, (1, chunk), 1)
            bias = jnp.where(position < len_ref[request], 0.0, MASKED)
            window = pl.ds(index * chunk, chunk)
            state = absorb(
                state, query, kv_ref[0, request, window], kv_ref[1, request, window], scale, bias
            )
        mean, level = finish(state, diagonal)
        out_ref[pl.ds(request * rows, rows), :] = mean.astype(jnp.bfloat16)
        level_ref[pl.ds(request, 1), :] = level


def place_kernel(
    scale,
    chunk,
    table_ref,
    place_ref,
    join_ref,
    q_ref,
    fresh_ref,
    arrived_ref,
    res_ref,
    res_level_ref,
    cache_ref,
    pay_ref,
):
    senders = arrived_ref.shape[0]
    _, slots, block_len, depth = cache_ref.shape
    dev_blocks = table_ref.shape[0] // senders
    steps, requests, group, _ = q_ref.shape
    rows = steps * group
    resident = requests - 1
    seq_index = place_ref[1]
    base = seq_index * slots

    def settle(sender, carry):
        def look(block, found):
            slot = table_ref[sender * dev_blocks + block] - base
            return jnp.where((slot >= 0) & (slot < slots), slot, found)

        found = lax.fori_loop(0, dev_blocks, look, 0, unroll=True)
        for part in range(2):
            cache_ref[part, found] = arrived_ref[sender, part]
        return carry

    lax.fori_loop(0, senders, settle, 0)
    diagonal = unit(rows)
    query = query_rows(q_ref, resident)
    state = absorb(
        empty_state(rows, depth),
        query,
        fresh_ref[0, resident],
        fresh_ref[1, resident],
        scale,
        fresh_bias(steps, group, resident, resident, join_ref[0], seq_index == 0),
    )
    per_chunk = chunk // block_len
    for index in range(senders // per_chunk):
        window = pl.ds(index * per_chunk, per_chunk)
        keys = arrived_ref[window, 0].reshape(chunk, depth)
        values = arrived_ref[window, 1].reshape(chunk, depth)
        state = absorb(state, query, keys, values, scale, None)
    mean, level = finish(state, diagonal)
    pay_ref[pl.ds(0, resident * rows), :] = res_ref[...]
    pay_ref[pl.ds(resident * rows, rows), :] = mean.astype(jnp.bfloat16)
    levels = [res_level_ref[pl.ds(request, 1), :] for request in range(resident)] + [level]
    pay_ref[pl.ds(requests * rows, 16), :] = tail_rows(levels)


def merged(flag, mine_ref, other_ref, request, requests, rows, diagonal):
    def ordered(window):
        mine = mine_ref[window, :].astype(jnp.float32)
        other = other_ref[window, :].astype(jnp.float32)
        return jnp.where(flag, mine, other), jnp.where(flag, other, mine)

    first_tail, second_tail = ordered(pl.ds(requests * rows, 16))

    def level_of(tail):
        level = tail[request * PIECES : request * PIECES + 1]
        for piece in range(1, PIECES):
            at = request * PIECES + piece
            level = level + tail[at : at + 1]
        return level

    first_level, second_level = level_of(first_tail), level_of(second_tail)
    top = jnp.maximum(first_level, second_level)
    first_weight = jnp.exp2(first_level - top)
    second_weight = jnp.exp2(second_level - top)
    total = first_weight + second_weight
    first_share = to_column(first_weight / total, diagonal)
    second_share = to_column(second_weight / total, diagonal)
    first, second = ordered(pl.ds(request * rows, rows))
    return first * first_share + second * second_share, top + jnp.log2(total)


def merge_kernel(requests, flag_ref, mine_ref, other_ref, out_ref):
    rows = mine_ref.shape[1]
    flag = flag_ref[0] == 0
    diagonal = unit(rows)
    levels = []
    for request in range(requests):
        mean, level = merged(flag, mine_ref, other_ref, request, requests, rows, diagonal)
        out_ref[pl.ds(request * rows, rows), :] = mean.astype(jnp.bfloat16)
        levels.append(level)
    out_ref[pl.ds(requests * rows, 16), :] = tail_rows(levels)


def final_kernel(flag_ref, join_ref, mine_ref, other_ref, out_ref):
    steps, requests, group, depth = out_ref.shape
    rows = mine_ref.shape[1]
    flag = flag_ref[0] == 0
    diagonal = unit(rows)
    for request in range(requests):
        mean, _ = merged(flag, mine_ref, other_ref, request, requests, rows, diagonal)
        if request == requests - 1:
            step = lax.broadcasted_iota(jnp.int32, (rows, depth), 0) // group
            mean = jnp.where(step >= join_ref[0], mean, 0.0)
        out_ref[:, request] = mean.reshape(steps, group, depth).astype(jnp.bfloat16)


def call(kernel, out_shape, in_specs, out_specs, cost, scratch=()):
    return pl.pallas_call(
        kernel,
        out_shape=out_shape,
        in_specs=in_specs,
        out_specs=out_specs,
        scratch_shapes=list(scratch),
        cost_estimate=pl.CostEstimate(flops=cost, bytes_accessed=cost // 128, transcendentals=0),
    )


def per_device(queries, new_kv, res_kv, prefill_kv, block_table, lengths, join_step):
    seq_index = lax.axis_index("seq")
    head_index = lax.axis_index("head")
    seq_count = lax.axis_size("seq")
    head_count = lax.axis_size("head")
    senders = seq_count * head_count
    steps, requests, group, depth = queries.shape
    rows = steps * group
    resident = res_kv.shape[1]
    res_rows = res_kv.shape[2]
    head_total = prefill_kv.shape[1]
    total_blocks = block_table.shape[0]
    dev_blocks = total_blocks // senders
    block_len = prefill_kv.shape[2] // dev_blocks
    slots = total_blocks // seq_count
    assert dev_blocks == seq_count and head_total == head_count and rows == depth
    assert seq_count & (seq_count - 1) == 0
    scale = LOG2E / math.sqrt(depth)
    bf16, f32 = jnp.bfloat16, jnp.float32
    place = jnp.stack([seq_index * head_count + head_index, seq_index]).astype(jnp.int32)
    blocks = prefill_kv.reshape(2, head_total, dev_blocks, block_len, depth)
    fresh = jnp.transpose(new_kv[:, :, :, 0], (0, 2, 1, 3))

    outgoing = call(
        functools.partial(pack_kernel, slots),
        jax.ShapeDtypeStruct((senders, 2, block_len, depth), bf16),
        [smem(), smem(), vmem()],
        vmem(),
        1 << 20,
    )(block_table, place, blocks)
    arrived = lax.all_to_all(outgoing, ("seq", "head"), split_axis=0, concat_axis=0, tiled=True)

    chunk = min(1024, res_rows)
    res_mean, res_level = call(
        functools.partial(resident_kernel, scale, chunk),
        (
            jax.ShapeDtypeStruct((resident * rows, depth), bf16),
            jax.ShapeDtypeStruct((resident, rows), f32),
        ),
        [smem(), smem(), vmem(), vmem(), anywhere()],
        (vmem(), vmem()),
        4 * resident * rows * res_rows * depth,
        [
            pltpu.VMEM((2, resident, res_rows, depth), bf16),
            pltpu.SemaphoreType.DMA((2, resident, res_rows // chunk)),
        ],
    )(lengths, place, queries, fresh, res_kv[:, :, :, 0])

    pay_shape = jax.ShapeDtypeStruct((requests * rows + 16, depth), bf16)
    cache, payload = call(
        functools.partial(place_kernel, scale, min(1024, senders * block_len)),
        (jax.ShapeDtypeStruct((2, slots, block_len, depth), bf16), pay_shape),
        [smem(), smem(), smem(), vmem(), vmem(), vmem(), vmem(), vmem()],
        (vmem(), vmem()),
        4 * rows * senders * block_len * depth,
    )(block_table, place, join_step, queries, fresh, arrived, res_mean, res_level)
    new_cache = cache.reshape(2, 1, slots * block_len, depth)

    bit = 1
    while bit < seq_count:
        pairs = [(index, index ^ bit) for index in range(seq_count)]
        other = lax.ppermute(payload, "seq", pairs)
        flag = ((seq_index // bit) % 2).astype(jnp.int32).reshape(1)
        bit *= 2
        if bit < seq_count:
            payload = call(
                functools.partial(merge_kernel, requests),
                pay_shape,
                [smem(), vmem(), vmem()],
                vmem(),
                1 << 20,
            )(flag, payload, other)
    attn_out = call(
        final_kernel,
        jax.ShapeDtypeStruct((steps, requests, group, depth), bf16),
        [smem(), smem(), vmem(), vmem()],
        vmem(),
        1 << 20,
    )(flag, join_step, payload, other)
    return (attn_out, new_cache)


def solution(mesh):
    in_specs = (
        P("groups", None, "head", None),
        P("groups", None, None, "head", None),
        P("groups", None, "seq", "head", None),
        P("groups", None, ("seq", "head"), None),
        P("groups"),
        P("groups"),
        P("groups"),
    )
    out_specs = (P("groups", None, "head", None), P("groups", "head", "seq", None))
    return jax.shard_map(
        per_device, mesh=mesh, in_specs=in_specs, out_specs=out_specs, check_vma=False
    )
```

time: 73.3 us -> 46.7 us (0.64)
  blocking collectives: 41.9 us -> 0 us
  waiting for transfers between devices: 0.04 us -> 16.3 us
  Pallas kernels: 0 us -> 15.3 us
  other arithmetic: 7.65 us -> 0.61 us
  local copies, waits for them, and re-layouts: 8.28 us -> 2.08 us
  matrix products: 5.95 us -> 0 us
  starting transfers between devices: 7.39 us -> 10.7 us
    all_gather x3 -> x0, blocking collectives: 41.9 us -> none  [merged_2(): everything = jax.tree.map(lambda part: lax.all_gather(part, axis), shard)]
    pallas_call x0 -> x5, Pallas kernels: none -> 15.3 us  [the longest x1 7.09 us: per_device(): call(functools.partial(resident_kernel, scale, chunk), (jax.ShapeDtypeStr...]
    ppermute x0 -> x2, waiting for transfers between devices: none -> 9.83 us  [per_device(): other = lax.ppermute(payload, 'seq', pairs)]
    all_to_all x1, waiting for transfers between devices: 0.04 us -> 6.52 us  [per_device(): lax.all_to_all(outgoing, ('seq', 'head'), split_axis=0, concat_axis=0, ti...]
    dot_general x8 -> x0, matrix products: 5.95 us -> none  [the longest x3 3.83 us: partial_softmax(): jnp.einsum('rd,pd->rp', query_rows, key_rows, preferred_element_type=jnp....]
    ppermute x0 -> x2, starting transfers between devices: none -> 3.29 us  [per_device(): other = lax.ppermute(payload, 'seq', pairs)]
    gather x5 -> x0, local copies, waits for them, and re-layouts: 2.65 us -> none  [the longest x2 0.68 us: per_device(): relaid = jnp.take(arrived, take_rows, axis=1)]
    reshape x8 -> x0, local copies, waits for them, and re-layouts: 2.11 us -> none  [the longest x2 0.87 us: per_device(): table_rows = block_table.reshape(senders, dev_blocks)]
  transfers between devices with their start and end apart: 1 -> 3, of which waited for: 0 -> 3; matrix products, arithmetic and copies ran while one was open for 17% -> 0% of each run, Pallas kernels for 0% -> 15%
where the time goes in v1:
time: 46.7 us; the launch traced here: 46.3 us
  waiting for transfers between devices  16.3 us (35%)
  Pallas kernels  15.3 us (33%)
  starting transfers between devices  10.7 us (23%)
  local copies, waits for them, and re-layouts  2.08 us (4%)
  between operations  1.31 us (3%)
  other arithmetic  0.61 us (1%)
    ppermute x2, waiting for transfers between devices, per_device(): other = lax.ppermute(payload, 'seq', pairs)  9.83 us
    all_to_all x1, starting transfers between devices, per_device(): lax.all_to_all(outgoing, ('seq', 'head'), split_axis=0, concat_axis=0, ti...  7.39 us
    pallas_call x1, Pallas kernels, per_device(): call(functools.partial(resident_kernel, scale, chunk), (jax.ShapeDtypeStr...  7.09 us
    all_to_all x1, waiting for transfers between devices, per_device(): lax.all_to_all(outgoing, ('seq', 'head'), split_axis=0, concat_axis=0, ti...  6.52 us
    ppermute x2, starting transfers between devices, per_device(): other = lax.ppermute(payload, 'seq', pairs)  3.29 us
    pallas_call x1, Pallas kernels, per_device(): call(functools.partial(place_kernel, scale, min(1024, senders * block_len...  2.73 us
    unnamed x6, local copies, waits for them, and re-layouts  2.08 us
    pallas_call x1, Pallas kernels, per_device(): call(functools.partial(pack_kernel, slots), jax.ShapeDtypeStruct((senders...  1.89 us
  transfers between devices with their start and end apart: 3, of which 3 were waited for; matrix products, arithmetic and copies ran while one was open for 0% of the time, Pallas kernels for 15%

profile of v1, /device:TPU:0, one launch (start us, length us, event | category | flops | bytes accessed | tf_op | source)
XLA Modules:
  0.0 46.3 jit_solution(16891779905936012576)
XLA Ops:
  0.6 0.6 %pad_add_fusion.place_ref = s32[2]{0:T(128)} fusion(s32[1]{0:T(128)} %bitcast.3, s32[1]{0:T(128)} %bitcast.2), kind=kLoop, calls=%fused_computation | loop fusion | flops 2 | bytes 16 | tf_op jit(solution)/shard_map/stack | solution.py:304
  1.2 1.9 %shard_map.86 = bf16[16,2,64,128]{3,2,1,0:T(8,128)(2,1)} custom-call(s32[64]{0:T(128)} %table_ref.3, s32[2]{0:T(128)} %pad_add_fusion.place_ref, bf16[2,4,4,64,128]{4,3,2,1,0:T(8,128)(2,1)} %bitcast.13), custom_call_target="tpu_custom_call" | custom-call | flops 1048576 | bytes 8192 | tf_op jit(solution)/shard_map/pallas_call | solution.py:308
  3.1 7.4 %all-to-all-start = ((bf16[16,2,64,128]{3,2,1,0:T(8,128)(2,1)}), bf16[16,2,64,128]{3,2,1,0:T(8,128)(2,1)S(1)}, u32[]{:S(2)}, u32[]{:S(2)}) async-start(bf16[16,2,64,128]{3,2,1,0:T(8,128)(2,1)} %shard_map.86), calls=%async_computation | async-start | bytes 1048576 | tf_op jit(solution)/shard_map/all_to_all | solution.py:315
  11.2 7.1 %shard_map.87 = (bf16[256,128]{1,0:T(8,128)(2,1)}, f32[2,128]{1,0:T(2,128)}) custom-call(s32[3]{0:T(128)} %len_ref.1, s32[2]{0:T(128)} %pad_add_fusion.place_ref, bf16[16,3,8,128]{3,2,1,0:T(8,128)(2,1)} %q_ref.3, bf16[2,3,16,128]{3,2,1,0:T(8,128)(2,1)} %bitcast.14, bf16[2,2,4096,128]{3,2,1,0:T(8,128)(2,1)} %bitcast.12), custom_call_target="tpu_custom_call" | custom-call | flops 536870912 | bytes 4194304 | tf_op jit(solution)/shard_map/pallas_call | solution.py:318
  18.3 6.5 %all-to-all-done.arrived_ref = bf16[16,2,64,128]{3,2,1,0:T(8,128)(2,1)S(1)} async-done(((bf16[16,2,64,128]{3,2,1,0:T(8,128)(2,1)}), bf16[16,2,64,128]{3,2,1,0:T(8,128)(2,1)S(1)}, u32[]{:S(2)}, u32[]{:S(2)}) %all-to-all-start) | async-done | bytes 524320 | tf_op jit(solution)/shard_map/all_to_all | solution.py:315
  24.8 0.0 copy-start
  24.8 0.8 %copy-done = bf16[16,2,64,128]{3,2,1,0:T(8,128)(2,1)} copy-done((bf16[16,2,64,128]{3,2,1,0:T(8,128)(2,1)}, bf16[16,2,64,128]{3,2,1,0:T(8,128)(2,1)S(1)}, u32[]{:S(2)}) %copy-start) | copy-done | bytes 524312
  25.6 2.7 %shard_map.88 = (bf16[2,16,64,128]{3,2,1,0:T(8,128)(2,1)}, bf16[400,128]{1,0:T(8,128)(2,1)}) custom-call(s32[64]{0:T(128)} %table_ref.3, s32[2]{0:T(128)} %pad_add_fusion.place_ref, s32[1]{0:T(128)S(6)} %copy.10.join_ref, bf16[16,3,8,128]{3,2,1,0:T(8,128)(2,1)} %q_ref.3, bf16[2,3,16,128]{3,2,1,0:T(8,128)(2,1)} %bitcast.15, bf16[16,2,64,128]{3,2,1,0:T(8,128)(2,1)} %copy-done, ...), custom_call_target="tpu_custom_call" | custom-call | flops 67108864 | bytes 524288 | tf_op jit(solution)/shard_map/pallas_call | solution.py:334
  28.3 1.1 %collective-permute-start = (bf16[400,128]{1,0:T(8,128)(2,1)}, bf16[400,128]{1,0:T(8,128)(2,1)S(1)}, u32[]{:S(2)}, u32[]{:S(2)}) collective-permute-start(bf16[400,128]{1,0:T(8,128)(2,1)} %get-tuple-element.8.mine_ref), channel_id=1, source_target_pairs={{0,4},{4,0},{8,12},{12,8},{1,5},{5,1},{9,13},{13,9},{2,6},{6,2},{1... | collective-permute-start | bytes 307208 | tf_op jit(solution)/shard_map/ppermute | solution.py:346
  29.5 4.0 %collective-permute-done.other_ref = bf16[400,128]{1,0:T(8,128)(2,1)S(1)} collective-permute-done((bf16[400,128]{1,0:T(8,128)(2,1)}, bf16[400,128]{1,0:T(8,128)(2,1)S(1)}, u32[]{:S(2)}, u32[]{:S(2)}) %collective-permute-start) | collective-permute-done | bytes 102432 | tf_op jit(solution)/shard_map/ppermute | solution.py:346
  33.5 0.0 copy-start.2
  33.5 0.6 %copy-done.2 = bf16[400,128]{1,0:T(8,128)(2,1)} copy-done((bf16[400,128]{1,0:T(8,128)(2,1)}, bf16[400,128]{1,0:T(8,128)(2,1)S(1)}, u32[]{:S(2)}) %copy-start.2) | copy-done | bytes 102424
  34.1 1.8 %shard_map.89.mine_ref = bf16[400,128]{1,0:T(8,128)(2,1)} custom-call(s32[1]{0:T(128)} %bitcast.1.flag_ref, bf16[400,128]{1,0:T(8,128)(2,1)} %get-tuple-element.8.mine_ref, bf16[400,128]{1,0:T(8,128)(2,1)} %copy-done.2), custom_call_target="tpu_custom_call" | custom-call | flops 1048576 | bytes 8192 | tf_op jit(solution)/shard_map/pallas_call | solution.py:350
  35.9 2.1 %collective-permute-start.1 = (bf16[400,128]{1,0:T(8,128)(2,1)}, bf16[400,128]{1,0:T(8,128)(2,1)S(1)}, u32[]{:S(2)}, u32[]{:S(2)}) collective-permute-start(bf16[400,128]{1,0:T(8,128)(2,1)} %shard_map.89.mine_ref), channel_id=1, source_target_pairs={{0,8},{4,12},{8,0},{12,4},{1,9},{5,13},{9,1},{13,5},{2,10},{6,14},... | collective-permute-start | bytes 307208 | tf_op jit(solution)/shard_map/ppermute | solution.py:346
  38.0 5.8 %collective-permute-done.1.other_ref = bf16[400,128]{1,0:T(8,128)(2,1)S(1)} collective-permute-done((bf16[400,128]{1,0:T(8,128)(2,1)}, bf16[400,128]{1,0:T(8,128)(2,1)S(1)}, u32[]{:S(2)}, u32[]{:S(2)}) %collective-permute-start.1) | collective-permute-done | bytes 102432 | tf_op jit(solution)/shard_map/ppermute | solution.py:346
  43.9 0.0 copy-start.1
  43.9 0.6 %copy-done.1 = bf16[400,128]{1,0:T(8,128)(2,1)} copy-done((bf16[400,128]{1,0:T(8,128)(2,1)}, bf16[400,128]{1,0:T(8,128)(2,1)S(1)}, u32[]{:S(2)}) %copy-start.1) | copy-done | bytes 102424
  44.5 1.8 %shard_map.90 = bf16[16,3,8,128]{3,2,1,0:T(8,128)(2,1)} custom-call(s32[1]{0:T(128)} %bitcast.flag_ref, s32[1]{0:T(128)S(6)} %copy.10.join_ref, bf16[400,128]{1,0:T(8,128)(2,1)} %shard_map.89.mine_ref, bf16[400,128]{1,0:T(8,128)(2,1)} %copy-done.1), custom_call_target="tpu_custom_call" | custom-call | flops 1048576 | bytes 8192 | tf_op jit(solution)/shard_map/pallas_call | solution.py:357
Async XLA Ops:
  3.1 21.7 %all-to-all-start = ((bf16[16,2,64,128]{3,2,1,0:T(8,128)(2,1)}), bf16[16,2,64,128]{3,2,1,0:T(8,128)(2,1)S(1)}, u32[]{:S(2)}, u32[]{:S(2)}) async-start(bf16[16,2,64,128]{3,2,1,0:T(8,128)(2,1)} %shard_map.86), calls=%async_computation | async-start | bytes 1048576 | tf_op jit(solution)/shard_map/all_to_all | solution.py:315
  24.8 0.8 %copy-start = (bf16[16,2,64,128]{3,2,1,0:T(8,128)(2,1)}, bf16[16,2,64,128]{3,2,1,0:T(8,128)(2,1)S(1)}, u32[]{:S(2)}) copy-start(bf16[16,2,64,128]{3,2,1,0:T(8,128)(2,1)S(1)} %all-to-all-done.arrived_ref) | copy-start | bytes 1572868
  28.3 5.1 %collective-permute-start = (bf16[400,128]{1,0:T(8,128)(2,1)}, bf16[400,128]{1,0:T(8,128)(2,1)S(1)}, u32[]{:S(2)}, u32[]{:S(2)}) collective-permute-start(bf16[400,128]{1,0:T(8,128)(2,1)} %get-tuple-element.8.mine_ref), channel_id=1, source_target_pairs={{0,4},{4,0},{8,12},{12,8},{1,5},{5,1},{9,13},{13,9},{2,6},{6,2},{1... | collective-permute-start | bytes 307208 | tf_op jit(solution)/shard_map/ppermute | solution.py:346
  33.5 0.6 %copy-start.2 = (bf16[400,128]{1,0:T(8,128)(2,1)}, bf16[400,128]{1,0:T(8,128)(2,1)S(1)}, u32[]{:S(2)}) copy-start(bf16[400,128]{1,0:T(8,128)(2,1)S(1)} %collective-permute-done.other_ref) | copy-start | bytes 307204
  35.9 8.0 %collective-permute-start.1 = (bf16[400,128]{1,0:T(8,128)(2,1)}, bf16[400,128]{1,0:T(8,128)(2,1)S(1)}, u32[]{:S(2)}, u32[]{:S(2)}) collective-permute-start(bf16[400,128]{1,0:T(8,128)(2,1)} %shard_map.89.mine_ref), channel_id=1, source_target_pairs={{0,8},{4,12},{8,0},{12,4},{1,9},{5,13},{9,1},{13,5},{2,10},{6,14},... | collective-permute-start | bytes 307208 | tf_op jit(solution)/shard_map/ppermute | solution.py:346
  43.9 0.6 %copy-start.1 = (bf16[400,128]{1,0:T(8,128)(2,1)}, bf16[400,128]{1,0:T(8,128)(2,1)S(1)}, u32[]{:S(2)}) copy-start(bf16[400,128]{1,0:T(8,128)(2,1)S(1)} %collective-permute-done.1.other_ref) | copy-start | bytes 307204

commit v2 on v1

v2 whole, which is shorter than its diff:
```python
import functools
import math

import jax
import jax.numpy as jnp
from jax import lax
from jax.experimental import pallas as pl
from jax.experimental.pallas import tpu as pltpu
from jax.sharding import PartitionSpec as P

FLOOR = -1e30
MASKED = -2e30
PIECES = 3
LOG2E = math.log2(math.e)


def vmem():
    return pl.BlockSpec(memory_space=pltpu.VMEM)


def smem():
    return pl.BlockSpec(memory_space=pltpu.SMEM)


def query_rows(q_ref, request):
    steps, _, group, depth = q_ref.shape
    wide = q_ref[:, request].astype(jnp.float32)
    return wide.reshape(steps * group, depth).astype(jnp.bfloat16)


def fresh_bias(steps, group, request, resident, joined, owner):
    rows = steps * group
    row_step = lax.broadcasted_iota(jnp.int32, (rows, steps), 0) // group
    key_step = lax.broadcasted_iota(jnp.int32, (rows, steps), 1)
    allowed = (key_step <= row_step) & owner
    if request >= resident:
        allowed = allowed & (key_step >= joined)
    return jnp.where(allowed, 0.0, MASKED)


def unit(rows):
    return lax.broadcasted_iota(jnp.int32, (rows, rows), 0) == lax.broadcasted_iota(
        jnp.int32, (rows, rows), 1
    )


def to_row(column, diagonal):
    return jnp.sum(jnp.where(diagonal, column, 0.0), axis=0, keepdims=True)


def to_column(row, diagonal):
    return jnp.sum(jnp.where(diagonal, row, 0.0), axis=1, keepdims=True)


def split(row):
    parts = []
    rest = row
    for _ in range(PIECES):
        part = rest.astype(jnp.bfloat16).astype(jnp.float32)
        parts.append(part)
        rest = rest - part
    return parts


def finish(state, diagonal):
    row_max, total, summed = state
    safe = jnp.where(total > 0.0, total, 1.0)
    return summed / safe, to_row(row_max + jnp.log2(safe), diagonal)


def tail_rows(levels):
    parts = [part for level in levels for part in split(level)]
    width = parts[0].shape[1]
    count = -(-len(parts) // 16) * 16
    parts.append(jnp.zeros((count - len(parts), width), jnp.float32))
    return jnp.concatenate(parts, axis=0).astype(jnp.bfloat16)


def lanes(wide, op):
    width = wide.shape[1]
    step = min(width, 128)
    out = wide[:, :step]
    for start in range(step, width, step):
        out = op(out, wide[:, start : start + step])
    return out


def attend(query, parts, scale, score_ref, copies=()):
    if copies:
        copies[0].wait()
    rows = query.shape[0]
    top = None
    start = 0
    for keys, _, bias in parts:
        count = keys.shape[0]
        scores = lax.dot_general(
            query, keys[...], (((1,), (1,)), ((), ())), preferred_element_type=jnp.float32
        )
        scores = scores * scale
        if bias is not None:
            scores = scores + bias
        score_ref[:, pl.ds(start, count)] = scores
        highest = lanes(scores, jnp.maximum)
        highest = jnp.max(highest, axis=1, keepdims=True) if count < 128 else highest
        top = highest if top is None else jnp.maximum(top, highest)
        start += -(-count // 128) * 128
    row_max = jnp.maximum(jnp.max(top, axis=1, keepdims=True), FLOOR)
    if copies:
        copies[1].wait()
    total = jnp.zeros((rows, 1), jnp.float32)
    summed = jnp.zeros((rows, parts[0][1].shape[1]), jnp.float32)
    start = 0
    for keys, values, _ in parts:
        count = keys.shape[0]
        weight = jnp.exp2(score_ref[:, pl.ds(start, count)] - row_max)
        total = total + jnp.sum(lanes(weight, jnp.add), axis=1, keepdims=True)
        summed = summed + jnp.dot(
            weight.astype(jnp.bfloat16), values[...], preferred_element_type=jnp.float32
        )
        start += -(-count // 128) * 128
    return row_max, total, summed


def pack_kernel(slots, table_ref, block_ref, send_ref, near_ref, far_ref):
    _, heads, dev_blocks, _, _ = block_ref.shape
    head_index = lax.axis_index("head")
    sender = lax.axis_index("seq") * heads + head_index
    for block in range(dev_blocks):
        shard = table_ref[sender * dev_blocks + block] // slots
        for head in range(heads):
            for part in range(2):
                send_ref[shard * heads + head, part] = block_ref[part, head, block]
    half = heads // 2
    for offset in range(heads):
        head = head_index ^ offset
        target, at = (near_ref, offset) if offset < half else (far_ref, offset - half)
        for part in range(2):
            target[at, part] = block_ref[part, head].reshape(target.shape[2:])


def resident_kernel(
    scale, len_ref, q_ref, fresh_ref, kv_hbm, out_ref, level_ref, kv_ref, score_ref, sems
):
    resident, length = kv_ref.shape[1], kv_ref.shape[2]
    copies = [
        [
            pltpu.make_async_copy(
                kv_hbm.at[part, request], kv_ref.at[part, request], sems.at[part, request]
            )
            for part in range(2)
        ]
        for request in range(resident)
    ]
    for pair in copies:
        for copy in pair:
            copy.start()
    steps, _, group, depth = q_ref.shape
    rows = steps * group
    diagonal = unit(rows)
    seq_index = lax.axis_index("seq")
    position = seq_index * length + lax.broadcasted_iota(jnp.int32, (1, length), 1)
    for request in range(resident):
        bias = jnp.where(position < len_ref[request], 0.0, MASKED)
        recent = fresh_bias(steps, group, request, resident, 0, seq_index == 0)
        state = attend(
            query_rows(q_ref, request),
            [
                (kv_ref.at[0, request], kv_ref.at[1, request], bias),
                (fresh_ref.at[0, request], fresh_ref.at[1, request], recent),
            ],
            scale,
            score_ref.at[request],
            copies[request],
        )
        mean, level = finish(state, diagonal)
        out_ref[pl.ds(request * rows, rows), :] = mean.astype(jnp.bfloat16)
        level_ref[pl.ds(request, 1), :] = level


def joining_kernel(scale, count, join_ref, q_ref, fresh_ref, res_ref, res_level_ref, *refs):
    sources, (pay_ref, score_ref) = refs[:count], refs[count:]
    steps, requests, group, depth = q_ref.shape
    rows = steps * group
    resident = requests - 1
    diagonal = unit(rows)
    seq_index = lax.axis_index("seq")
    recent = fresh_bias(steps, group, resident, resident, join_ref[0], seq_index == 0)
    parts = [(ref.at[0, 0], ref.at[0, 1], None) for ref in sources]
    parts.append((fresh_ref.at[0, resident], fresh_ref.at[1, resident], recent))
    state = attend(query_rows(q_ref, resident), parts, scale, score_ref)
    mean, level = finish(state, diagonal)
    step = lax.broadcasted_iota(jnp.int32, (rows, depth), 0) // group
    mean = jnp.where(step >= join_ref[0], mean, 0.0)
    pay_ref[pl.ds(0, resident * rows), :] = res_ref[...]
    pay_ref[pl.ds(resident * rows, rows), :] = mean.astype(jnp.bfloat16)
    levels = [res_level_ref[pl.ds(request, 1), :] for request in range(resident)] + [level]
    tail = tail_rows(levels)
    pay_ref[pl.ds(requests * rows, tail.shape[0]), :] = tail


def place_kernel(table_ref, arrived_ref, cache_ref):
    senders = arrived_ref.shape[0]
    slots = cache_ref.shape[1]
    dev_blocks = table_ref.shape[0] // senders
    base = lax.axis_index("seq") * slots

    def settle(sender, carry):
        def look(block, found):
            slot = table_ref[sender * dev_blocks + block] - base
            return jnp.where((slot >= 0) & (slot < slots), slot, found)

        found = lax.fori_loop(0, dev_blocks, look, 0, unroll=True)
        for part in range(2):
            cache_ref[part, found] = arrived_ref[sender, part]
        return carry

    lax.fori_loop(0, senders, settle, 0)


def final_kernel(count, *refs):
    pay_refs, (out_ref,) = refs[:count], refs[count:]
    steps, requests, group, depth = out_ref.shape
    rows = steps * group
    diagonal = unit(rows)
    seq_index = lax.axis_index("seq")
    tail = pl.ds(requests * rows, pay_refs[0].shape[0] - requests * rows)
    tails = [ref[tail, :].astype(jnp.float32) for ref in pay_refs]

    def level_of(rest, request):
        level = rest[request * PIECES : request * PIECES + 1]
        for at in range(request * PIECES + 1, (request + 1) * PIECES):
            level = level + rest[at : at + 1]
        return level

    def in_order(items):
        bit = 1
        while bit < count:
            swap = (seq_index & bit) != 0
            items = [
                jnp.where(swap, items[index ^ bit], items[index]) for index in range(len(items))
            ]
            bit *= 2
        return items

    for request in range(requests):
        levels = [level_of(rest, request) for rest in tails]
        top = functools.reduce(jnp.maximum, levels)
        weights = in_order([jnp.exp2(level - top) for level in levels])
        total = functools.reduce(jnp.add, weights)
        window = pl.ds(request * rows, rows)
        means = in_order([ref[window, :].astype(jnp.float32) for ref in pay_refs])
        result = None
        for mean, weight in zip(means, weights):
            term = mean * to_column(weight / total, diagonal)
            result = term if result is None else result + term
        out_ref[:, request] = result.reshape(steps, group, depth).astype(jnp.bfloat16)


def size_of(array):
    return math.prod(array.shape) * jnp.dtype(array.dtype).itemsize


def call(kernel, out_shape, in_specs, out_specs, flops, scratch=(), grant=0):
    def run(*operands):
        blocks = [
            array
            for array, spec in zip(operands, in_specs)
            if spec.memory_space is pltpu.VMEM
        ]
        blocks += jax.tree.leaves(out_shape)
        held = sum(size_of(array) for array in blocks)
        held += sum(size_of(ref) for ref in scratch if ref.memory_space is pltpu.VMEM)
        return pl.pallas_call(
            kernel,
            out_shape=out_shape,
            in_specs=in_specs,
            out_specs=out_specs,
            scratch_shapes=list(scratch),
            cost_estimate=pl.CostEstimate(
                flops=flops, bytes_accessed=held, transcendentals=0
            ),
            compiler_params=pltpu.CompilerParams(vmem_limit_bytes=max(held + (2 << 20), grant)),
        )(*operands)

    return run


def head_exchange(held, head_count):
    bit = head_count // 2
    while bit:
        pairs = [(index, index ^ bit) for index in range(head_count)]
        kept = [lower for lower, _ in held]
        kept += [lax.ppermute(upper, "head", pairs) for _, upper in held]
        bit //= 2
        if not bit:
            return kept
        held = [(part[:bit], part[bit:]) for part in kept]


def per_device(queries, new_kv, res_kv, prefill_kv, block_table, lengths, join_step):
    seq_count = lax.axis_size("seq")
    head_count = lax.axis_size("head")
    senders = seq_count * head_count
    steps, requests, group, depth = queries.shape
    rows = steps * group
    resident = res_kv.shape[1]
    res_rows = res_kv.shape[2]
    head_total, new_rows = prefill_kv.shape[1:3]
    total_blocks = block_table.shape[0]
    dev_blocks = total_blocks // senders
    block_len = new_rows // dev_blocks
    slots = total_blocks // seq_count
    assert dev_blocks == seq_count and head_total == head_count and rows == depth
    assert seq_count & (seq_count - 1) == 0 and head_count & (head_count - 1) == 0
    scale = LOG2E / math.sqrt(depth)
    bf16, f32 = jnp.bfloat16, jnp.float32
    blocks = prefill_kv.reshape(2, head_total, dev_blocks, block_len, depth)
    fresh = jnp.transpose(new_kv[:, :, :, 0], (0, 2, 1, 3))
    half_shape = jax.ShapeDtypeStruct((head_count // 2, 2, new_rows, depth), bf16)

    outgoing, near, far = call(
        functools.partial(pack_kernel, slots),
        (jax.ShapeDtypeStruct((senders, 2, block_len, depth), bf16), half_shape, half_shape),
        [smem(), vmem()],
        (vmem(), vmem(), vmem()),
        1 << 20,
    )(block_table, blocks)
    sources = head_exchange([(near, far)], head_count)
    arrived = lax.all_to_all(outgoing, ("seq", "head"), split_axis=0, concat_axis=0, tiled=True)

    padded = res_rows + -(-steps // 128) * 128
    res_mean, res_level = call(
        functools.partial(resident_kernel, scale),
        (
            jax.ShapeDtypeStruct((resident * rows, depth), bf16),
            jax.ShapeDtypeStruct((resident, rows), f32),
        ),
        [smem(), vmem(), vmem(), pl.BlockSpec(memory_space=pltpu.HBM)],
        (vmem(), vmem()),
        4 * resident * rows * res_rows * depth,
        [
            pltpu.VMEM((2, resident, res_rows, depth), bf16),
            pltpu.VMEM((resident, rows, padded), f32),
            pltpu.SemaphoreType.DMA((2, resident)),
        ],
        61 << 20,
    )(lengths, queries, fresh, res_kv[:, :, :, 0])

    padded = head_count * new_rows + -(-steps // 128) * 128
    payload = call(
        functools.partial(joining_kernel, scale, len(sources)),
        jax.ShapeDtypeStruct((requests * rows + 16 * -(-requests * PIECES // 16), depth), bf16),
        [smem(), vmem(), vmem(), vmem(), vmem()] + [vmem()] * len(sources),
        vmem(),
        4 * rows * head_count * new_rows * depth,
        [pltpu.VMEM((rows, padded), f32)],
    )(join_step, queries, fresh, res_mean, res_level, *sources)

    shares = [payload]
    for offset in range(1, seq_count):
        pairs = [(index, index ^ offset) for index in range(seq_count)]
        shares.append(lax.ppermute(payload, "seq", pairs))
    attn_out = call(
        functools.partial(final_kernel, seq_count),
        jax.ShapeDtypeStruct((steps, requests, group, depth), bf16),
        [vmem()] * seq_count,
        vmem(),
        1 << 20,
    )(*shares)

    cache = call(
        place_kernel,
        jax.ShapeDtypeStruct((2, slots, block_len, depth), bf16),
        [smem(), vmem()],
        vmem(),
        1 << 20,
    )(block_table, arrived)
    return (attn_out, cache.reshape(2, 1, slots * block_len, depth))


def solution(mesh):
    in_specs = (
        P("groups", None, "head", None),
        P("groups", None, None, "head", None),
        P("groups", None, "seq", "head", None),
        P("groups", None, ("seq", "head"), None),
        P("groups"),
        P("groups"),
        P("groups"),
    )
    out_specs = (P("groups", None, "head", None), P("groups", "head", "seq", None))
    return jax.shard_map(
        per_device, mesh=mesh, in_specs=in_specs, out_specs=out_specs, check_vma=False
    )
```

time: 46.7 us -> 48.6 us (1.041)
  Pallas kernels: 15.3 us -> 9.64 us
  starting transfers between devices: 10.7 us -> 14.2 us
  waiting for transfers between devices: 16.3 us -> 19.8 us
  local copies, waits for them, and re-layouts: 2.08 us -> 3.25 us
  other arithmetic: 0.61 us -> 0 us
    ppermute x2 -> x6, waiting for transfers between devices: 9.83 us -> 19.8 us  [the longest x3 11.5 us: head_exchange(): kept += [lax.ppermute(upper, 'head', pairs) for _, upper in held]]
    all_to_all x1, waiting for transfers between devices: 6.52 us -> 0.01 us  [per_device(): lax.all_to_all(outgoing, ('seq', 'head'), split_axis=0, concat_axis=0, ti...]
    pallas_call x5, Pallas kernels: 15.3 us -> 9.64 us  [run(): pl.pallas_call(kernel, out_shape=out_shape, in_specs=in_specs, out_specs=...]
    ppermute x2 -> x6, starting transfers between devices: 3.29 us -> 6.81 us  [the longest x3 4.74 us: per_device(): shares.append(lax.ppermute(payload, 'seq', pairs))]
    unnamed x6 -> x14, local copies, waits for them, and re-layouts: 2.08 us -> 3.22 us
    another operation x1 -> x0, other arithmetic: 0.61 us -> none  [per_device(): jnp.stack([seq_index * head_count + head_index, seq_index])]
  transfers between devices with their start and end apart: 3 -> 7, of which waited for: 3 -> 3; matrix products, arithmetic and copies ran while one was open for 0% -> 0% of each run, Pallas kernels for 15% -> 14%
where the time goes in v2:
time: 48.6 us; the launch traced here: 48.3 us
  waiting for transfers between devices  19.8 us (41%)
  starting transfers between devices  14.2 us (29%)
  Pallas kernels  9.64 us (20%)
  local copies, waits for them, and re-layouts  3.25 us (7%)
  between operations  1.39 us (3%)
    ppermute x3, waiting for transfers between devices, head_exchange(): kept += [lax.ppermute(upper, 'head', pairs) for _, upper in held]  11.5 us
    pallas_call x5, Pallas kernels, run(): pl.pallas_call(kernel, out_shape=out_shape, in_specs=in_specs, out_specs=...  9.64 us
    ppermute x3, waiting for transfers between devices, per_device(): shares.append(lax.ppermute(payload, 'seq', pairs))  8.32 us
    all_to_all x1, starting transfers between devices, per_device(): lax.all_to_all(outgoing, ('seq', 'head'), split_axis=0, concat_axis=0, ti...  7.39 us
    ppermute x3, starting transfers between devices, per_device(): shares.append(lax.ppermute(payload, 'seq', pairs))  4.74 us
    unnamed x14, local copies, waits for them, and re-layouts  3.22 us
    ppermute x3, starting transfers between devices, head_exchange(): kept += [lax.ppermute(upper, 'head', pairs) for _, upper in held]  2.07 us
  transfers between devices with their start and end apart: 7, of which 3 were waited for; matrix products, arithmetic and copies ran while one was open for 0% of the time, Pallas kernels for 14%

profile of v2, /device:TPU:0, one launch (start us, length us, event | category | flops | bytes accessed | tf_op | source)
XLA Modules:
  0.0 48.3 jit_solution(5889581361515055673)
XLA Ops:
  0.6 0.0 copy-start.5
  0.6 0.0 copy-start
  0.6 1.0 %copy-done = bf16[2,4,256,128]{3,2,1,0:T(8,128)(2,1)S(1)} copy-done((bf16[2,4,256,128]{3,2,1,0:T(8,128)(2,1)S(1)}, bf16[2,4,256,128]{3,2,1,0:T(8,128)(2,1)}, u32[]{:S(2)}) %copy-start) | copy-done | bytes 524312
  1.7 0.0 copy-start.4
  1.7 0.7 %copy-done.4 = s32[64]{0:T(128)S(1)} copy-done((s32[64]{0:T(128)S(1)}, s32[64]{0:T(128)}, u32[]{:S(2)}) %copy-start.4) | copy-done | bytes 280
  2.3 0.0 copy-start.1
  2.3 0.0 copy-start.2
  2.3 1.4 %shard_map.87 = (bf16[16,2,64,128]{3,2,1,0:T(8,128)(2,1)}, bf16[2,2,256,128]{3,2,1,0:T(8,128)(2,1)S(1)}, bf16[2,2,256,128]{3,2,1,0:T(8,128)(2,1)S(1)}) custom-call(s32[64]{0:T(128)S(1)} %copy-done.4, bf16[2,4,4,64,128]{4,3,2,1,0:T(8,128)(2,1)S(1)} %bitcast.8), custom_call_target="tpu_custom_call" | custom-call | flops 1048576 | bytes 1572864 | tf_op jit(solution)/shard_map/pallas_call | solution.py:273
  3.8 7.4 %all-to-all-start = ((bf16[16,2,64,128]{3,2,1,0:T(8,128)(2,1)}), bf16[16,2,64,128]{3,2,1,0:T(8,128)(2,1)S(1)}, u32[]{:S(2)}, u32[]{:S(2)}) async-start(bf16[16,2,64,128]{3,2,1,0:T(8,128)(2,1)} %get-tuple-element.11), calls=%async_computation | async-start | bytes 1048576 | tf_op jit(solution)/shard_map/all_to_all | solution.py:329
  11.2 1.9 %collective-permute-start = (bf16[2,2,256,128]{3,2,1,0:T(8,128)(2,1)S(1)}, bf16[2,2,256,128]{3,2,1,0:T(8,128)(2,1)S(1)}, u32[]{:S(2)}, u32[]{:S(2)}) collective-permute-start(bf16[2,2,256,128]{3,2,1,0:T(8,128)(2,1)S(1)} %get-tuple-element.10), channel_id=1, source_target_pairs={{0,2},{1,3},{2,0},{3,1},{4,6},{5,7},{6,4},{7,5},{8,10},{9,11},{10,... | collective-permute-start | bytes 786440 | tf_op jit(solution)/shard_map/ppermute | solution.py:293
  13.1 0.1 collective-permute-start.1
  13.2 11.5 %collective-permute-done = bf16[2,2,256,128]{3,2,1,0:T(8,128)(2,1)S(1)} collective-permute-done((bf16[2,2,256,128]{3,2,1,0:T(8,128)(2,1)S(1)}, bf16[2,2,256,128]{3,2,1,0:T(8,128)(2,1)S(1)}, u32[]{:S(2)}, u32[]{:S(2)}) %collective-permute-start) | collective-permute-done | bytes 262176 | tf_op jit(solution)/shard_map/ppermute | solution.py:293
  24.7 0.1 collective-permute-start.2
  25.4 5.0 %shard_map.86 = (bf16[256,128]{1,0:T(8,128)(2,1)}, f32[2,128]{1,0:T(2,128)}) custom-call(s32[3]{0:T(128)} %len_ref.1, bf16[16,3,8,128]{3,2,1,0:T(8,128)(2,1)} %q_ref.3, bf16[2,3,16,128]{3,2,1,0:T(8,128)(2,1)} %bitcast.9, bf16[2,2,4096,128]{3,2,1,0:T(8,128)(2,1)} %bitcast.11), custom_call_target="tpu_custom_call" | custom-call | flops 536870912 | bytes 8709120 | tf_op jit(solution)/shard_map/pallas_call | solution.py:273
  30.4 0.0 collective-permute-done.1.refs_2_
  30.4 0.0 collective-permute-done.2.refs_3_
  30.4 0.0 copy-done.1
  30.4 0.0 copy-done.2
  30.4 0.0 copy-start.3
  30.4 0.8 %copy-done.3 = bf16[256,128]{1,0:T(8,128)(2,1)S(1)} copy-done((bf16[256,128]{1,0:T(8,128)(2,1)S(1)}, bf16[256,128]{1,0:T(8,128)(2,1)}, u32[]{:S(2)}) %copy-start.3) | copy-done | bytes 65560
  31.3 0.0 copy-start.6
  31.3 0.7 %copy-done.6 = f32[2,128]{1,0:T(2,128)S(1)} copy-done((f32[2,128]{1,0:T(2,128)S(1)}, f32[2,128]{1,0:T(2,128)}, u32[]{:S(2)}) %copy-start.6) | copy-done | bytes 1048
  31.9 0.6 %shard_map.88.refs_0_ = bf16[400,128]{1,0:T(8,128)(2,1)S(1)} custom-call(s32[1]{0:T(128)S(6)} %copy.10.join_ref, bf16[16,3,8,128]{3,2,1,0:T(8,128)(2,1)S(1)} %copy-done.1, bf16[2,3,16,128]{3,2,1,0:T(8,128)(2,1)S(1)} %bitcast.10, bf16[256,128]{1,0:T(8,128)(2,1)S(1)} %copy-done.3, f32[2,128]{1,0:T(2,128)S(1)} %copy-done.6, ...), custom_call_target="tpu_custom_call" | custom-call | flops 67108864 | bytes 1405952 | tf_op jit(solution)/shard_map/pallas_call | solution.py:273
  32.6 2.0 %collective-permute-start.3 = (bf16[400,128]{1,0:T(8,128)(2,1)S(1)}, bf16[400,128]{1,0:T(8,128)(2,1)S(1)}, u32[]{:S(2)}, u32[]{:S(2)}) collective-permute-start(bf16[400,128]{1,0:T(8,128)(2,1)S(1)} %shard_map.88.refs_0_), channel_id=1, source_target_pairs={{0,4},{4,0},{8,12},{12,8},{1,5},{5,1},{9,13},{13,9},{2,6},{6,2},{1... | collective-permute-start | bytes 307208 | tf_op jit(solution)/shard_map/ppermute | solution.py:362
  34.6 2.7 %collective-permute-start.4 = (bf16[400,128]{1,0:T(8,128)(2,1)S(1)}, bf16[400,128]{1,0:T(8,128)(2,1)S(1)}, u32[]{:S(2)}, u32[]{:S(2)}) collective-permute-start(bf16[400,128]{1,0:T(8,128)(2,1)S(1)} %shard_map.88.refs_0_), channel_id=1, source_target_pairs={{0,8},{4,12},{8,0},{12,4},{1,9},{5,13},{9,1},{13,5},{2,10},{6,14},... | collective-permute-start | bytes 307208 | tf_op jit(solution)/shard_map/ppermute | solution.py:362
  37.3 0.0 collective-permute-start.5
  37.3 0.8 %collective-permute-done.3.refs_1_ = bf16[400,128]{1,0:T(8,128)(2,1)S(1)} collective-permute-done((bf16[400,128]{1,0:T(8,128)(2,1)S(1)}, bf16[400,128]{1,0:T(8,128)(2,1)S(1)}, u32[]{:S(2)}, u32[]{:S(2)}) %collective-permute-start.3) | collective-permute-done | bytes 102432 | tf_op jit(solution)/shard_map/ppermute | solution.py:362
  38.2 7.5 %collective-permute-done.4.refs_2_ = bf16[400,128]{1,0:T(8,128)(2,1)S(1)} collective-permute-done((bf16[400,128]{1,0:T(8,128)(2,1)S(1)}, bf16[400,128]{1,0:T(8,128)(2,1)S(1)}, u32[]{:S(2)}, u32[]{:S(2)}) %collective-permute-start.4) | collective-permute-done | bytes 102432 | tf_op jit(solution)/shard_map/ppermute | solution.py:362
  45.6 0.0 collective-permute-done.5.refs_3_
  45.7 1.0 %shard_map.89 = bf16[16,3,8,128]{3,2,1,0:T(8,128)(2,1)} custom-call(bf16[400,128]{1,0:T(8,128)(2,1)S(1)} %shard_map.88.refs_0_, bf16[400,128]{1,0:T(8,128)(2,1)S(1)} %collective-permute-done.3.refs_1_, bf16[400,128]{1,0:T(8,128)(2,1)S(1)} %collective-permute-done.4.refs_2_, bf16[400,128]{1,0:T(8,128)(2,1)S(1)} %collective-permute-done.5.refs_3_), custom_call_target="tpu_custom_call" | custom-call | flops 1048576 | bytes 507904 | tf_op jit(solution)/shard_map/pallas_call | solution.py:273
  46.7 0.0 all-to-all-done.arrived_ref
  46.7 0.0 copy-done.5
  46.7 1.6 %shard_map.90 = bf16[2,16,64,128]{3,2,1,0:T(8,128)(2,1)} custom-call(s32[64]{0:T(128)S(1)} %copy-done.5, bf16[16,2,64,128]{3,2,1,0:T(8,128)(2,1)S(1)} %all-to-all-done.arrived_ref), custom_call_target="tpu_custom_call" | custom-call | flops 1048576 | bytes 1048576 | tf_op jit(solution)/shard_map/pallas_call | solution.py:273
  (2 shorter events, 0.0 us)
Async XLA Ops:
  0.6 46.1 %copy-start.5 = (s32[64]{0:T(128)S(1)}, s32[64]{0:T(128)}, u32[]{:S(2)}) copy-start(s32[64]{0:T(128)} %table_ref.3) | copy-start | bytes 772
  0.6 1.0 %copy-start = (bf16[2,4,256,128]{3,2,1,0:T(8,128)(2,1)S(1)}, bf16[2,4,256,128]{3,2,1,0:T(8,128)(2,1)}, u32[]{:S(2)}) copy-start(bf16[2,4,256,128]{3,2,1,0:T(8,128)(2,1)} %param.10) | copy-start | bytes 1572868
  1.7 0.7 %copy-start.4 = (s32[64]{0:T(128)S(1)}, s32[64]{0:T(128)}, u32[]{:S(2)}) copy-start(s32[64]{0:T(128)} %table_ref.3) | copy-start | bytes 772
  2.3 28.1 %copy-start.1 = (bf16[16,3,8,128]{3,2,1,0:T(8,128)(2,1)S(1)}, bf16[16,3,8,128]{3,2,1,0:T(8,128)(2,1)}, u32[]{:S(2)}) copy-start(bf16[16,3,8,128]{3,2,1,0:T(8,128)(2,1)} %q_ref.3) | copy-start | bytes 294916
  2.3 28.1 %copy-start.2 = (bf16[2,16,3,1,128]{4,1,3,2,0:T(8,128)(2,1)S(1)}, bf16[2,16,3,1,128]{4,1,3,2,0:T(8,128)(2,1)}, u32[]{:S(2)}) copy-start(bf16[2,16,3,1,128]{4,1,3,2,0:T(8,128)(2,1)} %param.8) | copy-start | bytes 73732
  3.8 42.9 %all-to-all-start = ((bf16[16,2,64,128]{3,2,1,0:T(8,128)(2,1)}), bf16[16,2,64,128]{3,2,1,0:T(8,128)(2,1)S(1)}, u32[]{:S(2)}, u32[]{:S(2)}) async-start(bf16[16,2,64,128]{3,2,1,0:T(8,128)(2,1)} %get-tuple-element.11), calls=%async_computation | async-start | bytes 1048576 | tf_op jit(solution)/shard_map/all_to_all | solution.py:329
  11.2 13.5 %collective-permute-start = (bf16[2,2,256,128]{3,2,1,0:T(8,128)(2,1)S(1)}, bf16[2,2,256,128]{3,2,1,0:T(8,128)(2,1)S(1)}, u32[]{:S(2)}, u32[]{:S(2)}) collective-permute-start(bf16[2,2,256,128]{3,2,1,0:T(8,128)(2,1)S(1)} %get-tuple-element.10), channel_id=1, source_target_pairs={{0,2},{1,3},{2,0},{3,1},{4,6},{5,7},{6,4},{7,5},{8,10},{9,11},{10,... | collective-permute-start | bytes 786440 | tf_op jit(solution)/shard_map/ppermute | solution.py:293
  13.1 17.3 %collective-permute-start.1 = (bf16[1,2,256,128]{3,2,1,0:T(8,128)(2,1)S(1)}, bf16[1,2,256,128]{3,2,1,0:T(8,128)(2,1)S(1)}, u32[]{:S(2)}, u32[]{:S(2)}) collective-permute-start(bf16[1,2,256,128]{3,2,1,0:T(8,128)(2,1)S(1)} %get-tuple-element.16), channel_id=1, source_target_pairs={{0,1},{1,0},{2,3},{3,2},{4,5},{5,4},{6,7},{7,6},{8,9},{9,8},{10,11... | collective-permute-start | bytes 393224 | tf_op jit(solution)/shard_map/ppermute | solution.py:293
  24.7 5.7 %collective-permute-start.2 = (bf16[1,2,256,128]{3,2,1,0:T(8,128)(2,1)S(1)}, bf16[1,2,256,128]{3,2,1,0:T(8,128)(2,1)S(1)}, u32[]{:S(2)}, u32[]{:S(2)}) collective-permute-start(bf16[1,2,256,128]{3,2,1,0:T(8,128)(2,1)S(1)} %get-tuple-element.14), channel_id=1, source_target_pairs={{0,1},{1,0},{2,3},{3,2},{4,5},{5,4},{6,7},{7,6},{8,9},{9,8},{10,11... | collective-permute-start | bytes 393224 | tf_op jit(solution)/shard_map/ppermute | solution.py:293
  30.4 0.8 %copy-start.3 = (bf16[256,128]{1,0:T(8,128)(2,1)S(1)}, bf16[256,128]{1,0:T(8,128)(2,1)}, u32[]{:S(2)}) copy-start(bf16[256,128]{1,0:T(8,128)(2,1)} %get-tuple-element.7.res_ref) | copy-start | bytes 196612
  31.3 0.7 %copy-start.6 = (f32[2,128]{1,0:T(2,128)S(1)}, f32[2,128]{1,0:T(2,128)}, u32[]{:S(2)}) copy-start(f32[2,128]{1,0:T(2,128)} %get-tuple-element.8.res_level_ref) | copy-start | bytes 3076
  32.6 5.6 %collective-permute-start.3 = (bf16[400,128]{1,0:T(8,128)(2,1)S(1)}, bf16[400,128]{1,0:T(8,128)(2,1)S(1)}, u32[]{:S(2)}, u32[]{:S(2)}) collective-permute-start(bf16[400,128]{1,0:T(8,128)(2,1)S(1)} %shard_map.88.refs_0_), channel_id=1, source_target_pairs={{0,4},{4,0},{8,12},{12,8},{1,5},{5,1},{9,13},{13,9},{2,6},{6,2},{1... | collective-permute-start | bytes 307208 | tf_op jit(solution)/shard_map/ppermute | solution.py:362
  34.6 11.0 %collective-permute-start.4 = (bf16[400,128]{1,0:T(8,128)(2,1)S(1)}, bf16[400,128]{1,0:T(8,128)(2,1)S(1)}, u32[]{:S(2)}, u32[]{:S(2)}) collective-permute-start(bf16[400,128]{1,0:T(8,128)(2,1)S(1)} %shard_map.88.refs_0_), channel_id=1, source_target_pairs={{0,8},{4,12},{8,0},{12,4},{1,9},{5,13},{9,1},{13,5},{2,10},{6,14},... | collective-permute-start | bytes 307208 | tf_op jit(solution)/shard_map/ppermute | solution.py:362
  37.3 8.3 %collective-permute-start.5 = (bf16[400,128]{1,0:T(8,128)(2,1)S(1)}, bf16[400,128]{1,0:T(8,128)(2,1)S(1)}, u32[]{:S(2)}, u32[]{:S(2)}) collective-permute-start(bf16[400,128]{1,0:T(8,128)(2,1)S(1)} %shard_map.88.refs_0_), channel_id=1, source_target_pairs={{0,12},{4,8},{8,4},{12,0},{1,13},{5,9},{9,5},{13,1},{2,14},{6,10},... | collective-permute-start | bytes 307208 | tf_op jit(solution)/shard_map/ppermute | solution.py:362

commit v3 on v2

--- a/solution.py
+++ b/solution.py
@@ -8,9 +8,11 @@
 from jax.experimental.pallas import tpu as pltpu
 from jax.sharding import PartitionSpec as P
 
+
 FLOOR = -1e30
 MASKED = -2e30
 PIECES = 3
+PACK_FLOPS = 1 << 33
 LOG2E = math.log2(math.e)
 
 
@@ -85,9 +87,7 @@
     return out
 
 
-def attend(query, parts, scale, score_ref, copies=()):
-    if copies:
-        copies[0].wait()
+def attend(query, parts, scale, score_ref):
     rows = query.shape[0]
     top = None
     start = 0
@@ -105,8 +105,6 @@
         top = highest if top is None else jnp.maximum(top, highest)
         start += -(-count // 128) * 128
     row_max = jnp.maximum(jnp.max(top, axis=1, keepdims=True), FLOOR)
-    if copies:
-        copies[1].wait()
     total = jnp.zeros((rows, 1), jnp.float32)
     summed = jnp.zeros((rows, parts[0][1].shape[1]), jnp.float32)
     start = 0
@@ -121,40 +119,19 @@
     return row_max, total, summed
 
 
-def pack_kernel(slots, table_ref, block_ref, send_ref, near_ref, far_ref):
+def pack_kernel(slots, table_ref, block_ref, send_ref):
     _, heads, dev_blocks, _, _ = block_ref.shape
-    head_index = lax.axis_index("head")
-    sender = lax.axis_index("seq") * heads + head_index
+    sender = lax.axis_index("seq") * heads + lax.axis_index("head")
     for block in range(dev_blocks):
         shard = table_ref[sender * dev_blocks + block] // slots
         for head in range(heads):
             for part in range(2):
                 send_ref[shard * heads + head, part] = block_ref[part, head, block]
-    half = heads // 2
-    for offset in range(heads):
-        head = head_index ^ offset
-        target, at = (near_ref, offset) if offset < half else (far_ref, offset - half)
-        for part in range(2):
-            target[at, part] = block_ref[part, head].reshape(target.shape[2:])
-
-
-def resident_kernel(
-    scale, len_ref, q_ref, fresh_ref, kv_hbm, out_ref, level_ref, kv_ref, score_ref, sems
-):
+
+
+def resident_kernel(scale, len_ref, q_ref, fresh_ref, kv_ref, out_ref, level_ref, score_ref):
     resident, length = kv_ref.shape[1], kv_ref.shape[2]
-    copies = [
-        [
-            pltpu.make_async_copy(
-                kv_hbm.at[part, request], kv_ref.at[part, request], sems.at[part, request]
-            )
-            for part in range(2)
-        ]
-        for request in range(resident)
-    ]
-    for pair in copies:
-        for copy in pair:
-            copy.start()
-    steps, _, group, depth = q_ref.shape
+    steps, _, group, _ = q_ref.shape
     rows = steps * group
     diagonal = unit(rows)
     seq_index = lax.axis_index("seq")
@@ -170,14 +147,15 @@
             ],
             scale,
             score_ref.at[request],
-            copies[request],
         )
         mean, level = finish(state, diagonal)
         out_ref[pl.ds(request * rows, rows), :] = mean.astype(jnp.bfloat16)
         level_ref[pl.ds(request, 1), :] = level
 
 
-def joining_kernel(scale, count, join_ref, q_ref, fresh_ref, res_ref, res_level_ref, *refs):
+def joining_kernel(
+    scale, count, join_ref, q_ref, fresh_ref, res_ref, res_level_ref, prefill_ref, *refs
+):
     sources, (pay_ref, score_ref) = refs[:count], refs[count:]
     steps, requests, group, depth = q_ref.shape
     rows = steps * group
@@ -185,7 +163,9 @@
     diagonal = unit(rows)
     seq_index = lax.axis_index("seq")
     recent = fresh_bias(steps, group, resident, resident, join_ref[0], seq_index == 0)
-    parts = [(ref.at[0, 0], ref.at[0, 1], None) for ref in sources]
+    head_index = lax.axis_index("head")
+    parts = [(prefill_ref.at[0, head_index], prefill_ref.at[1, head_index], None)]
+    parts += [(ref.at[0, 0], ref.at[1, 0], None) for ref in sources]
     parts.append((fresh_ref.at[0, resident], fresh_ref.at[1, resident], recent))
     state = attend(query_rows(q_ref, resident), parts, scale, score_ref)
     mean, level = finish(state, diagonal)
@@ -217,50 +197,61 @@
     lax.fori_loop(0, senders, settle, 0)
 
 
-def final_kernel(count, *refs):
-    pay_refs, (out_ref,) = refs[:count], refs[count:]
+def merged(bit, mine_ref, other_ref, request, requests, rows, diagonal):
+    first_here = (lax.axis_index("seq") & bit) == 0
+    tail = pl.ds(requests * rows, mine_ref.shape[0] - requests * rows)
+
+    def level_of(ref):
+        rest = ref[tail, :].astype(jnp.float32)
+        at = request * PIECES
+        level = rest[at : at + 1]
+        for piece in range(1, PIECES):
+            level = level + rest[at + piece : at + piece + 1]
+        return level
+
+    def ordered(mine, other):
+        return jnp.where(first_here, mine, other), jnp.where(first_here, other, mine)
+
+    first_level, second_level = ordered(level_of(mine_ref), level_of(other_ref))
+    top = jnp.maximum(first_level, second_level)
+    first_weight = jnp.exp2(first_level - top)
+    second_weight = jnp.exp2(second_level - top)
+    total = first_weight + second_weight
+    window = pl.ds(request * rows, rows)
+    first, second = ordered(
+        mine_ref[window, :].astype(jnp.float32), other_ref[window, :].astype(jnp.float32)
+    )
+    mean = first * to_column(first_weight / total, diagonal)
+    mean = mean + second * to_column(second_weight / total, diagonal)
+    return mean, top + jnp.log2(total)
+
+
+def merge_kernel(bit, requests, mine_ref, other_ref, out_ref):
+    rows = mine_ref.shape[1]
+    diagonal = unit(rows)
+    levels = []
+    for request in range(requests):
+        mean, level = merged(bit, mine_ref, other_ref, request, requests, rows, diagonal)
+        out_ref[pl.ds(request * rows, rows), :] = mean.astype(jnp.bfloat16)
+        levels.append(level)
+    tail = tail_rows(levels)
+    out_ref[pl.ds(requests * rows, tail.shape[0]), :] = tail
+
+
+def final_kernel(bit, mine_ref, other_ref, out_ref):
     steps, requests, group, depth = out_ref.shape
     rows = steps * group
     diagonal = unit(rows)
-    seq_index = lax.axis_index("seq")
-    tail = pl.ds(requests * rows, pay_refs[0].shape[0] - requests * rows)
-    tails = [ref[tail, :].astype(jnp.float32) for ref in pay_refs]
-
-    def level_of(rest, request):
-        level = rest[request * PIECES : request * PIECES + 1]
-        for at in range(request * PIECES + 1, (request + 1) * PIECES):
-            level = level + rest[at : at + 1]
-        return level
-
-    def in_order(items):
-        bit = 1
-        while bit < count:
-            swap = (seq_index & bit) != 0
-            items = [
-                jnp.where(swap, items[index ^ bit], items[index]) for index in range(len(items))
-            ]
-            bit *= 2
-        return items
-
     for request in range(requests):
-        levels = [level_of(rest, request) for rest in tails]
-        top = functools.reduce(jnp.maximum, levels)
-        weights = in_order([jnp.exp2(level - top) for level in levels])
-        total = functools.reduce(jnp.add, weights)
-        window = pl.ds(request * rows, rows)
-        means = in_order([ref[window, :].astype(jnp.float32) for ref in pay_refs])
-        result = None
-        for mean, weight in zip(means, weights):
-            term = mean * to_column(weight / total, diagonal)
-            result = term if result is None else result + term
-        out_ref[:, request] = result.reshape(steps, group, depth).astype(jnp.bfloat16)
+        mean, _ = merged(bit, mine_ref, other_ref, request, requests, rows, diagonal)
+        out_ref[:, request] = mean.reshape(steps, group, depth).astype(jnp.bfloat16)
 
 
 def size_of(array):
     return math.prod(array.shape) * jnp.dtype(array.dtype).itemsize
 
 
-def call(kernel, out_shape, in_specs, out_specs, flops, scratch=(), grant=0):
+def call(kernel, out_shape, in_specs, out_specs, flops, scratch=()):
     def run(*operands):
         blocks = [
             array
@@ -279,22 +270,30 @@
             cost_estimate=pl.CostEstimate(
                 flops=flops, bytes_accessed=held, transcendentals=0
             ),
-            compiler_params=pltpu.CompilerParams(vmem_limit_bytes=max(held + (2 << 20), grant)),
+            compiler_params=pltpu.CompilerParams(vmem_limit_bytes=held + (2 << 20)),
         )(*operands)
 
     return run
 
 
-def head_exchange(held, head_count):
+def halves(array, index):
+    half = array.shape[1] // 2
+    mine = (index // half) % 2
+    return [
+        lax.dynamic_slice_in_dim(array, place * half, half, 1) for place in (mine, 1 - mine)
+    ]
+
+
+def head_exchange(prefill, head_index, head_count):
+    held = [prefill]
     bit = head_count // 2
     while bit:
         pairs = [(index, index ^ bit) for index in range(head_count)]
-        kept = [lower for lower, _ in held]
-        kept += [lax.ppermute(upper, "head", pairs) for _, upper in held]
+        split_up = [halves(part, head_index) for part in held]
+        sent = [lax.ppermute(other, "head", pairs) for _, other in split_up]
+        held = [mine for mine, _ in split_up] + sent
         bit //= 2
-        if not bit:
-            return kept
-        held = [(part[:bit], part[bit:]) for part in kept]
+    return held[1:]
 
 
 def per_device(queries, new_kv, res_kv, prefill_kv, block_table, lengths, join_step):
@@ -316,17 +315,17 @@
     bf16, f32 = jnp.bfloat16, jnp.float32
     blocks = prefill_kv.reshape(2, head_total, dev_blocks, block_len, depth)
     fresh = jnp.transpose(new_kv[:, :, :, 0], (0, 2, 1, 3))
-    half_shape = jax.ShapeDtypeStruct((head_count // 2, 2, new_rows, depth), bf16)
-
-    outgoing, near, far = call(
+    sources = head_exchange(prefill_kv, lax.axis_index("head"), head_count)
+    outgoing = call(
         functools.partial(pack_kernel, slots),
-        (jax.ShapeDtypeStruct((senders, 2, block_len, depth), bf16), half_shape, half_shape),
+        jax.ShapeDtypeStruct((senders, 2, block_len, depth), bf16),
         [smem(), vmem()],
-        (vmem(), vmem(), vmem()),
-        1 << 20,
+        vmem(),
+        PACK_FLOPS,
     )(block_table, blocks)
-    sources = head_exchange([(near, far)], head_count)
-    arrived = lax.all_to_all(outgoing, ("seq", "head"), split_axis=0, concat_axis=0, tiled=True)
+    arrived = lax.all_to_all(
+        outgoing, ("seq", "head"), split_axis=0, concat_axis=0, tiled=True
+    )
 
     padded = res_rows + -(-steps // 128) * 128
     res_mean, res_level = call(
@@ -335,38 +334,45 @@
             jax.ShapeDtypeStruct((resident * rows, depth), bf16),
             jax.ShapeDtypeStruct((resident, rows), f32),
         ),
-        [smem(), vmem(), vmem(), pl.BlockSpec(memory_space=pltpu.HBM)],
+        [smem(), vmem(), vmem(), vmem()],
         (vmem(), vmem()),
         4 * resident * rows * res_rows * depth,
         [
-            pltpu.VMEM((2, resident, res_rows, depth), bf16),
             pltpu.VMEM((resident, rows, padded), f32),
-            pltpu.SemaphoreType.DMA((2, resident)),
         ],
-        61 << 20,
     )(lengths, queries, fresh, res_kv[:, :, :, 0])
 
     padded = head_count * new_rows + -(-steps // 128) * 128
     payload = call(
         functools.partial(joining_kernel, scale, len(sources)),
         jax.ShapeDtypeStruct((requests * rows + 16 * -(-requests * PIECES // 16), depth), bf16),
-        [smem(), vmem(), vmem(), vmem(), vmem()] + [vmem()] * len(sources),
+        [smem()] + [vmem()] * (5 + len(sources)),
         vmem(),
         4 * rows * head_count * new_rows * depth,
         [pltpu.VMEM((rows, padded), f32)],
-    )(join_step, queries, fresh, res_mean, res_level, *sources)
-
-    shares = [payload]
-    for offset in range(1, seq_count):
-        pairs = [(index, index ^ offset) for index in range(seq_count)]
-        shares.append(lax.ppermute(payload, "seq", pairs))
+    )(join_step, queries, fresh, res_mean, res_level, prefill_kv, *sources)
+
+    bit = 1
+    while bit < seq_count:
+        pairs = [(index, index ^ bit) for index in range(seq_count)]
+        last = 2 * bit >= seq_count
+        other = lax.ppermute(payload, "seq", pairs)
+        if not last:
+            payload = call(
+                functools.partial(merge_kernel, bit, requests),
+                jax.ShapeDtypeStruct(payload.shape, bf16),
+                [vmem(), vmem()],
+                vmem(),
+                1 << 20,
+            )(payload, other)
+        bit *= 2
     attn_out = call(
-        functools.partial(final_kernel, seq_count),
+        functools.partial(final_kernel, bit // 2),
         jax.ShapeDtypeStruct((steps, requests, group, depth), bf16),
-        [vmem()] * seq_count,
+        [vmem(), vmem()],
         vmem(),
         1 << 20,
-    )(*shares)
+    )(payload, other)
 
     cache = call(
         place_kernel,
@@ -389,6 +395,7 @@
         P("groups"),
     )
     out_specs = (P("groups", None, "head", None), P("groups", "head", "seq", None))
+
     return jax.shard_map(
         per_device, mesh=mesh, in_specs=in_specs, out_specs=out_specs, check_vma=False
     )

time: 48.6 us -> 47.5 us (0.977)
  Pallas kernels: 9.64 us -> 7.4 us
  local copies, waits for them, and re-layouts: 3.25 us -> 3.94 us
    pallas_call x5 -> x6, Pallas kernels: 9.64 us -> 7.4 us  [run(): pl.pallas_call(kernel, out_shape=out_shape, in_specs=in_specs, out_specs=...]
    unnamed x14 -> x16, local copies, waits for them, and re-layouts: 3.22 us -> 3.89 us
    ppermute x6 -> x5, waiting for transfers between devices: 19.8 us -> 20 us  [the longest x3 11.4 us: head_exchange(): sent = [lax.ppermute(other, 'head', pairs) for _, other in split_up]]
    ppermute x6 -> x5, starting transfers between devices: 6.81 us -> 6.9 us  [the longest x2 4.8 us: per_device(): other = lax.ppermute(payload, 'seq', pairs)]
  transfers between devices with their start and end apart: 7 -> 6, of which waited for: 3 -> 3; matrix products, arithmetic and copies ran while one was open for 0% -> 0% of each run, Pallas kernels for 14% -> 9%
where the time goes in v3:
time: 47.5 us; the launch traced here: 47.2 us
  waiting for transfers between devices  20 us (42%)
  starting transfers between devices  14.4 us (30%)
  Pallas kernels  7.4 us (16%)
  local copies, waits for them, and re-layouts  3.94 us (8%)
  between operations  1.45 us (3%)
    ppermute x3, waiting for transfers between devices, head_exchange(): sent = [lax.ppermute(other, 'head', pairs) for _, other in split_up]  11.4 us
    ppermute x2, waiting for transfers between devices, per_device(): other = lax.ppermute(payload, 'seq', pairs)  8.59 us
    all_to_all x1, starting transfers between devices, per_device(): lax.all_to_all(outgoing, ('seq', 'head'), split_axis=0, concat_axis=0, ti...  7.52 us
    pallas_call x6, Pallas kernels, run(): pl.pallas_call(kernel, out_shape=out_shape, in_specs=in_specs, out_specs=...  7.4 us
    ppermute x2, starting transfers between devices, per_device(): other = lax.ppermute(payload, 'seq', pairs)  4.8 us
    unnamed x16, local copies, waits for them, and re-layouts  3.89 us
    ppermute x3, starting transfers between devices, head_exchange(): sent = [lax.ppermute(other, 'head', pairs) for _, other in split_up]  2.09 us
  transfers between devices with their start and end apart: 6, of which 3 were waited for; matrix products, arithmetic and copies ran while one was open for 0% of the time, Pallas kernels for 9%

profile of v3, /device:TPU:0, one launch (start us, length us, event | category | flops | bytes accessed | tf_op | source)
XLA Modules:
  0.0 47.2 jit_solution(11138771136512057617)
XLA Ops:
  0.6 0.0 copy-start.1
  0.6 1.0 %copy-done.1 = bf16[2,4,256,128]{3,2,1,0:T(8,128)(2,1)S(1)} copy-done((bf16[2,4,256,128]{3,2,1,0:T(8,128)(2,1)S(1)}, bf16[2,4,256,128]{3,2,1,0:T(8,128)(2,1)}, u32[]{:S(2)}) %copy-start.1) | copy-done | bytes 524312
  1.7 0.0 copy-start.6
  1.7 0.7 %copy-done.6 = s32[64]{0:T(128)S(1)} copy-done((s32[64]{0:T(128)S(1)}, s32[64]{0:T(128)}, u32[]{:S(2)}) %copy-start.6) | copy-done | bytes 280
  2.3 0.0 copy-start.2
  2.3 0.0 copy-start.3
  2.3 0.0 copy-start.4
  2.3 0.0 copy-start.5
  2.3 1.4 %shard_map.90 = bf16[16,2,64,128]{3,2,1,0:T(8,128)(2,1)} custom-call(s32[64]{0:T(128)S(1)} %copy-done.6, bf16[2,4,4,64,128]{4,3,2,1,0:T(8,128)(2,1)S(1)} %bitcast.9), custom_call_target="tpu_custom_call" | custom-call | flops 8589934592 | bytes 1048576 | tf_op jit(solution)/shard_map/pallas_call | solution.py:264
  3.7 0.0 copy-start.7
  3.7 7.5 %all-to-all-start = ((bf16[16,2,64,128]{3,2,1,0:T(8,128)(2,1)}), bf16[16,2,64,128]{3,2,1,0:T(8,128)(2,1)S(1)}, u32[]{:S(2)}, u32[]{:S(2)}) async-start(bf16[16,2,64,128]{3,2,1,0:T(8,128)(2,1)} %shard_map.90), calls=%async_computation | async-start | bytes 1048576 | tf_op jit(solution)/shard_map/all_to_all | solution.py:326
  11.3 0.0 copy-done.2
  11.3 2.0 %collective-permute-start = (bf16[2,2,256,128]{3,2,1,0:T(8,128)(2,1)S(1)}, bf16[2,2,256,128]{3,2,1,0:T(8,128)(2,1)S(1)}, u32[]{:S(2)}, u32[]{:S(2)}) collective-permute-start(bf16[2,2,256,128]{3,2,1,0:T(8,128)(2,1)S(1)} %constant_dynamic-slice_fusion.3), channel_id=1, source_target_pairs={{0,2},{1,3},{2,0},{3,1},{4,6},{5,7},{6,4},{7,5},{8,10},{9,11},{10,... | collective-permute-start | bytes 786440 | tf_op jit(solution)/shard_map/ppermute | solution.py:293
  13.3 0.1 collective-permute-start.1
  13.4 11.4 %collective-permute-done = bf16[2,2,256,128]{3,2,1,0:T(8,128)(2,1)S(1)} collective-permute-done((bf16[2,2,256,128]{3,2,1,0:T(8,128)(2,1)S(1)}, bf16[2,2,256,128]{3,2,1,0:T(8,128)(2,1)S(1)}, u32[]{:S(2)}, u32[]{:S(2)}) %collective-permute-start) | collective-permute-done | bytes 262176 | tf_op jit(solution)/shard_map/ppermute | solution.py:293
  24.8 0.1 collective-permute-start.2
  25.5 0.0 copy-done.3
  25.5 0.0 copy-done.4
  25.5 0.0 copy-done.5
  25.5 0.0 copy-start
  25.5 2.2 %copy-done = bf16[2,2,4096,1,128]{4,2,3,1,0:T(8,128)(2,1)S(1)} copy-done((bf16[2,2,4096,1,128]{4,2,3,1,0:T(8,128)(2,1)S(1)}, bf16[2,2,4096,1,128]{4,2,3,1,0:T(8,128)(2,1)}, u32[]{:S(2)}) %copy-start) | copy-done | bytes 4194328
  27.7 2.7 %shard_map.86 = (bf16[256,128]{1,0:T(8,128)(2,1)S(1)}, f32[2,128]{1,0:T(2,128)S(1)}) custom-call(s32[3]{0:T(128)S(1)} %copy-done.5, bf16[16,3,8,128]{3,2,1,0:T(8,128)(2,1)S(1)} %copy-done.3, bf16[2,3,16,128]{3,2,1,0:T(8,128)(2,1)S(1)} %bitcast.10, bf16[2,2,4096,128]{3,2,1,0:T(8,128)(2,1)S(1)} %bitcast.8), custom_call_target="tpu_custom_call" | custom-call | flops 536870912 | bytes 8709120 | tf_op jit(solution)/shard_map/pallas_call | solution.py:264
  30.5 0.0 collective-permute-done.1.refs_1_
  30.5 0.0 collective-permute-done.2.refs_2_
  30.5 0.7 %shard_map.87.mine_ref = bf16[400,128]{1,0:T(8,128)(2,1)S(1)} custom-call(s32[1]{0:T(128)S(6)} %copy.10.join_ref, bf16[16,3,8,128]{3,2,1,0:T(8,128)(2,1)S(1)} %copy-done.3, bf16[2,3,16,128]{3,2,1,0:T(8,128)(2,1)S(1)} %bitcast.11, bf16[256,128]{1,0:T(8,128)(2,1)S(1)} %get-tuple-element.4.res_ref, f32[2,128]{1,0:T(2,128)S(1)} %get-tuple-element.5.res_level_ref, ...), custom_call_target="tpu_custom_call" | custom-call | flops 67108864 | bytes 1799168 | tf_op jit(solution)/shard_map/pallas_call | solution.py:264
  31.1 2.0 %collective-permute-start.3 = (bf16[400,128]{1,0:T(8,128)(2,1)S(1)}, bf16[400,128]{1,0:T(8,128)(2,1)S(1)}, u32[]{:S(2)}, u32[]{:S(2)}) collective-permute-start(bf16[400,128]{1,0:T(8,128)(2,1)S(1)} %shard_map.87.mine_ref), channel_id=1, source_target_pairs={{0,4},{4,0},{8,12},{12,8},{1,5},{5,1},{9,13},{13,9},{2,6},{6,2},{1... | collective-permute-start | bytes 307208 | tf_op jit(solution)/shard_map/ppermute | solution.py:359
  33.2 3.6 %collective-permute-done.3.other_ref = bf16[400,128]{1,0:T(8,128)(2,1)S(1)} collective-permute-done((bf16[400,128]{1,0:T(8,128)(2,1)S(1)}, bf16[400,128]{1,0:T(8,128)(2,1)S(1)}, u32[]{:S(2)}, u32[]{:S(2)}) %collective-permute-start.3) | collective-permute-done | bytes 102432 | tf_op jit(solution)/shard_map/ppermute | solution.py:359
  36.7 0.2 shard_map.88.mine_ref
  36.9 2.8 %collective-permute-start.4 = (bf16[400,128]{1,0:T(8,128)(2,1)S(1)}, bf16[400,128]{1,0:T(8,128)(2,1)S(1)}, u32[]{:S(2)}, u32[]{:S(2)}) collective-permute-start(bf16[400,128]{1,0:T(8,128)(2,1)S(1)} %shard_map.88.mine_ref), channel_id=1, source_target_pairs={{0,8},{4,12},{8,0},{12,4},{1,9},{5,13},{9,1},{13,5},{2,10},{6,14},... | collective-permute-start | bytes 307208 | tf_op jit(solution)/shard_map/ppermute | solution.py:359
  39.7 5.0 %collective-permute-done.4.other_ref = bf16[400,128]{1,0:T(8,128)(2,1)S(1)} collective-permute-done((bf16[400,128]{1,0:T(8,128)(2,1)S(1)}, bf16[400,128]{1,0:T(8,128)(2,1)S(1)}, u32[]{:S(2)}, u32[]{:S(2)}) %collective-permute-start.4) | collective-permute-done | bytes 102432 | tf_op jit(solution)/shard_map/ppermute | solution.py:359
  44.7 0.8 %shard_map.89 = bf16[16,3,8,128]{3,2,1,0:T(8,128)(2,1)} custom-call(bf16[400,128]{1,0:T(8,128)(2,1)S(1)} %shard_map.88.mine_ref, bf16[400,128]{1,0:T(8,128)(2,1)S(1)} %collective-permute-done.4.other_ref), custom_call_target="tpu_custom_call" | custom-call | flops 1048576 | bytes 303104 | tf_op jit(solution)/shard_map/pallas_call | solution.py:264
  45.6 0.0 all-to-all-done.arrived_ref
  45.6 0.0 copy-done.7
  45.6 1.6 %shard_map.91 = bf16[2,16,64,128]{3,2,1,0:T(8,128)(2,1)} custom-call(s32[64]{0:T(128)S(1)} %copy-done.7, bf16[16,2,64,128]{3,2,1,0:T(8,128)(2,1)S(1)} %all-to-all-done.arrived_ref), custom_call_target="tpu_custom_call" | custom-call | flops 1048576 | bytes 1048576 | tf_op jit(solution)/shard_map/pallas_call | solution.py:264
  (3 shorter events, 0.1 us)
Async XLA Ops:
  0.6 1.0 %copy-start.1 = (bf16[2,4,256,128]{3,2,1,0:T(8,128)(2,1)S(1)}, bf16[2,4,256,128]{3,2,1,0:T(8,128)(2,1)}, u32[]{:S(2)}) copy-start(bf16[2,4,256,128]{3,2,1,0:T(8,128)(2,1)} %prefill_ref.1) | copy-start | bytes 1572868
  1.7 0.7 %copy-start.6 = (s32[64]{0:T(128)S(1)}, s32[64]{0:T(128)}, u32[]{:S(2)}) copy-start(s32[64]{0:T(128)} %table_ref.3) | copy-start | bytes 772
  2.3 9.0 %copy-start.2 = (bf16[2,4,256,128]{3,2,1,0:T(8,128)(2,1)S(1)}, bf16[2,4,256,128]{3,2,1,0:T(8,128)(2,1)}, u32[]{:S(2)}) copy-start(bf16[2,4,256,128]{3,2,1,0:T(8,128)(2,1)} %prefill_ref.1) | copy-start | bytes 1572868
  2.3 23.2 %copy-start.3 = (bf16[16,3,8,128]{3,2,1,0:T(8,128)(2,1)S(1)}, bf16[16,3,8,128]{3,2,1,0:T(8,128)(2,1)}, u32[]{:S(2)}) copy-start(bf16[16,3,8,128]{3,2,1,0:T(8,128)(2,1)} %q_ref.3) | copy-start | bytes 294916
  2.3 23.2 %copy-start.4 = (bf16[2,16,3,1,128]{4,1,3,2,0:T(8,128)(2,1)S(1)}, bf16[2,16,3,1,128]{4,1,3,2,0:T(8,128)(2,1)}, u32[]{:S(2)}) copy-start(bf16[2,16,3,1,128]{4,1,3,2,0:T(8,128)(2,1)} %param.8) | copy-start | bytes 73732
  2.3 23.2 %copy-start.5 = (s32[3]{0:T(128)S(1)}, s32[3]{0:T(128)}, u32[]{:S(2)}) copy-start(s32[3]{0:T(128)} %len_ref.1) | copy-start | bytes 40
  3.7 41.9 %copy-start.7 = (s32[64]{0:T(128)S(1)}, s32[64]{0:T(128)}, u32[]{:S(2)}) copy-start(s32[64]{0:T(128)} %table_ref.3) | copy-start | bytes 772
  3.7 41.9 %all-to-all-start = ((bf16[16,2,64,128]{3,2,1,0:T(8,128)(2,1)}), bf16[16,2,64,128]{3,2,1,0:T(8,128)(2,1)S(1)}, u32[]{:S(2)}, u32[]{:S(2)}) async-start(bf16[16,2,64,128]{3,2,1,0:T(8,128)(2,1)} %shard_map.90), calls=%async_computation | async-start | bytes 1048576 | tf_op jit(solution)/shard_map/all_to_all | solution.py:326
  11.3 13.4 %collective-permute-start = (bf16[2,2,256,128]{3,2,1,0:T(8,128)(2,1)S(1)}, bf16[2,2,256,128]{3,2,1,0:T(8,128)(2,1)S(1)}, u32[]{:S(2)}, u32[]{:S(2)}) collective-permute-start(bf16[2,2,256,128]{3,2,1,0:T(8,128)(2,1)S(1)} %constant_dynamic-slice_fusion.3), channel_id=1, source_target_pairs={{0,2},{1,3},{2,0},{3,1},{4,6},{5,7},{6,4},{7,5},{8,10},{9,11},{10,... | collective-permute-start | bytes 786440 | tf_op jit(solution)/shard_map/ppermute | solution.py:293
  13.3 17.2 %collective-permute-start.1 = (bf16[2,1,256,128]{3,2,1,0:T(8,128)(2,1)S(1)}, bf16[2,1,256,128]{3,2,1,0:T(8,128)(2,1)S(1)}, u32[]{:S(2)}, u32[]{:S(2)}) collective-permute-start(bf16[2,1,256,128]{3,2,1,0:T(8,128)(2,1)S(1)} %constant_dynamic-slice_fusion.1), channel_id=1, source_target_pairs={{0,1},{1,0},{2,3},{3,2},{4,5},{5,4},{6,7},{7,6},{8,9},{9,8},{10,11... | collective-permute-start | bytes 393224 | tf_op jit(solution)/shard_map/ppermute | solution.py:293
  24.8 5.7 %collective-permute-start.2 = (bf16[2,1,256,128]{3,2,1,0:T(8,128)(2,1)S(1)}, bf16[2,1,256,128]{3,2,1,0:T(8,128)(2,1)S(1)}, u32[]{:S(2)}, u32[]{:S(2)}) collective-permute-start(bf16[2,1,256,128]{3,2,1,0:T(8,128)(2,1)S(1)} %get-tuple-element.8), channel_id=1, source_target_pairs={{0,1},{1,0},{2,3},{3,2},{4,5},{5,4},{6,7},{7,6},{8,9},{9,8},{10,11... | collective-permute-start | bytes 393224 | tf_op jit(solution)/shard_map/ppermute | solution.py:293
  25.5 2.2 %copy-start = (bf16[2,2,4096,1,128]{4,2,3,1,0:T(8,128)(2,1)S(1)}, bf16[2,2,4096,1,128]{4,2,3,1,0:T(8,128)(2,1)}, u32[]{:S(2)}) copy-start(bf16[2,2,4096,1,128]{4,2,3,1,0:T(8,128)(2,1)} %param.9) | copy-start | bytes 12582916
  31.1 5.6 %collective-permute-start.3 = (bf16[400,128]{1,0:T(8,128)(2,1)S(1)}, bf16[400,128]{1,0:T(8,128)(2,1)S(1)}, u32[]{:S(2)}, u32[]{:S(2)}) collective-permute-start(bf16[400,128]{1,0:T(8,128)(2,1)S(1)} %shard_map.87.mine_ref), channel_id=1, source_target_pairs={{0,4},{4,0},{8,12},{12,8},{1,5},{5,1},{9,13},{13,9},{2,6},{6,2},{1... | collective-permute-start | bytes 307208 | tf_op jit(solution)/shard_map/ppermute | solution.py:359
  36.9 7.8 %collective-permute-start.4 = (bf16[400,128]{1,0:T(8,128)(2,1)S(1)}, bf16[400,128]{1,0:T(8,128)(2,1)S(1)}, u32[]{:S(2)}, u32[]{:S(2)}) collective-permute-start(bf16[400,128]{1,0:T(8,128)(2,1)S(1)} %shard_map.88.mine_ref), channel_id=1, source_target_pairs={{0,8},{4,12},{8,0},{12,4},{1,9},{5,13},{9,1},{13,5},{2,10},{6,14},... | collective-permute-start | bytes 307208 | tf_op jit(solution)/shard_map/ppermute | solution.py:359

commit v4 on v3

--- a/solution.py
+++ b/solution.py
@@ -22,6 +22,14 @@
 
 def smem():
     return pl.BlockSpec(memory_space=pltpu.SMEM)
+
+
+def hbm():
+    return pl.BlockSpec(memory_space=pltpu.HBM)
+
+
+def in_hbm(array):
+    return pltpu.with_memory_space_constraint(array, pltpu.HBM)
 
 
 def query_rows(q_ref, request):
@@ -87,7 +95,9 @@
     return out
 
 
-def attend(query, parts, scale, score_ref):
+def attend(query, parts, scale, score_ref, copies=()):
+    if copies:
+        copies[0].wait()
     rows = query.shape[0]
     top = None
     start = 0
@@ -105,6 +115,8 @@
         top = highest if top is None else jnp.maximum(top, highest)
         start += -(-count // 128) * 128
     row_max = jnp.maximum(jnp.max(top, axis=1, keepdims=True), FLOOR)
+    if copies:
+        copies[1].wait()
     total = jnp.zeros((rows, 1), jnp.float32)
     summed = jnp.zeros((rows, parts[0][1].shape[1]), jnp.float32)
     start = 0
@@ -119,25 +131,75 @@
     return row_max, total, summed
 
 
-def pack_kernel(slots, table_ref, block_ref, send_ref):
-    _, heads, dev_blocks, _, _ = block_ref.shape
-    sender = lax.axis_index("seq") * heads + lax.axis_index("head")
+def pack_kernel(
+    slots,
+    table_hbm,
+    block_hbm,
+    send_ref,
+    far_ref,
+    send_near_ref,
+    near_ref,
+    table_ref,
+    sems,
+):
+    _, heads, dev_blocks, _, _ = block_hbm.shape
+    head_index = lax.axis_index("head")
+    sender = lax.axis_index("seq") * heads + head_index
+    half = heads // 2
+    table_copy = pltpu.make_async_copy(table_hbm, table_ref, sems.at[0])
+    table_copy.start()
+    far = (1 - head_index // half) * half
+    quarter = half // 2
+    step = (head_index // quarter) % 2 * quarter
+    windows = (
+        (far, half, far_ref),
+        (half - far + quarter - step, quarter, send_near_ref),
+        (half - far + step, quarter, near_ref),
+    )
+    copies = [
+        pltpu.make_async_copy(block_hbm.at[:, pl.ds(start, size)], target, sems.at[1 + index])
+        for index, (start, size, target) in enumerate(windows)
+    ]
+    for copy in copies:
+        copy.start()
+    table_copy.wait()
     for block in range(dev_blocks):
         shard = table_ref[sender * dev_blocks + block] // slots
-        for head in range(heads):
-            for part in range(2):
-                send_ref[shard * heads + head, part] = block_ref[part, head, block]
-
-
-def resident_kernel(scale, len_ref, q_ref, fresh_ref, kv_ref, out_ref, level_ref, score_ref):
+        for part in range(2):
+            copy = pltpu.make_async_copy(
+                block_hbm.at[part, :, block],
+                send_ref.at[pl.ds(shard * heads, heads), part],
+                sems.at[4 + 2 * block + part],
+            )
+            copy.start()
+            copies.append(copy)
+    for copy in copies:
+        copy.wait()
+
+
+def resident_kernel(
+    scale, len_ref, q_ref, fresh_ref, kv_hbm, out_ref, level_ref, kv_ref, score_ref, sems
+):
     resident, length = kv_ref.shape[1], kv_ref.shape[2]
+    copies = [
+        [
+            pltpu.make_async_copy(
+                kv_hbm.at[part, request], kv_ref.at[part, request], sems.at[part, request]
+            )
+            for part in range(2)
+        ]
+        for request in range(resident)
+    ]
+    for pair in copies:
+        for copy in pair:
+            copy.start()
     steps, _, group, _ = q_ref.shape
     rows = steps * group
     diagonal = unit(rows)
     seq_index = lax.axis_index("seq")
     position = seq_index * length + lax.broadcasted_iota(jnp.int32, (1, length), 1)
     for request in range(resident):
-        bias = jnp.where(position < len_ref[request], 0.0, MASKED)
+        bias = jnp.where(position < len_ref[:, request : request + 1], 0.0, MASKED)
         recent = fresh_bias(steps, group, request, resident, 0, seq_index == 0)
         state = attend(
             query_rows(q_ref, request),
@@ -147,30 +209,21 @@
             ],
             scale,
             score_ref.at[request],
+            copies[request],
         )
         mean, level = finish(state, diagonal)
         out_ref[pl.ds(request * rows, rows), :] = mean.astype(jnp.bfloat16)
         level_ref[pl.ds(request, 1), :] = level
 
 
-def joining_kernel(
-    scale, count, join_ref, q_ref, fresh_ref, res_ref, res_level_ref, prefill_ref, *refs
-):
+def joining_kernel(scale, count, q_ref, res_ref, res_level_ref, *refs):
     sources, (pay_ref, score_ref) = refs[:count], refs[count:]
-    steps, requests, group, depth = q_ref.shape
+    steps, requests, group, _ = q_ref.shape
     rows = steps * group
     resident = requests - 1
-    diagonal = unit(rows)
-    seq_index = lax.axis_index("seq")
-    recent = fresh_bias(steps, group, resident, resident, join_ref[0], seq_index == 0)
-    head_index = lax.axis_index("head")
-    parts = [(prefill_ref.at[0, head_index], prefill_ref.at[1, head_index], None)]
-    parts += [(ref.at[0, 0], ref.at[1, 0], None) for ref in sources]
-    parts.append((fresh_ref.at[0, resident], fresh_ref.at[1, resident], recent))
+    parts = [(ref.at[0, 0], ref.at[1, 0], None) for ref in sources]
     state = attend(query_rows(q_ref, resident), parts, scale, score_ref)
-    mean, level = finish(state, diagonal)
-    step = lax.broadcasted_iota(jnp.int32, (rows, depth), 0) // group
-    mean = jnp.where(step >= join_ref[0], mean, 0.0)
+    mean, level = finish(state, unit(rows))
     pay_ref[pl.ds(0, resident * rows), :] = res_ref[...]
     pay_ref[pl.ds(resident * rows, rows), :] = mean.astype(jnp.bfloat16)
     levels = [res_level_ref[pl.ds(request, 1), :] for request in range(resident)] + [level]
@@ -197,45 +250,73 @@
     lax.fori_loop(0, senders, settle, 0)
 
 
+def blend(first, second, diagonal):
+    top = jnp.maximum(first[1], second[1])
+    first_weight = jnp.exp2(first[1] - top)
+    second_weight = jnp.exp2(second[1] - top)
+    total = first_weight + second_weight
+    mean = first[0] * to_column(first_weight / total, diagonal)
+    mean = mean + second[0] * to_column(second_weight / total, diagonal)
+    return mean, top + jnp.log2(total)
+
+
 def merged(bit, mine_ref, other_ref, request, requests, rows, diagonal):
     first_here = (lax.axis_index("seq") & bit) == 0
     tail = pl.ds(requests * rows, mine_ref.shape[0] - requests * rows)
-
-    def level_of(ref):
+    window = pl.ds(request * rows, rows)
+
+    def share(ref):
         rest = ref[tail, :].astype(jnp.float32)
         at = request * PIECES
         level = rest[at : at + 1]
         for piece in range(1, PIECES):
             level = level + rest[at + piece : at + piece + 1]
-        return level
-
-    def ordered(mine, other):
-        return jnp.where(first_here, mine, other), jnp.where(first_here, other, mine)
-
-    first_level, second_level = ordered(level_of(mine_ref), level_of(other_ref))
-    top = jnp.maximum(first_level, second_level)
-    first_weight = jnp.exp2(first_level - top)
-    second_weight = jnp.exp2(second_level - top)
-    total = first_weight + second_weight
-    window = pl.ds(request * rows, rows)
-    first, second = ordered(
-        mine_ref[window, :].astype(jnp.float32), other_ref[window, :].astype(jnp.float32)
-    )
-    mean = first * to_column(first_weight / total, diagonal)
-    mean = mean + second * to_column(second_weight / total, diagonal)
-    return mean, top + jnp.log2(total)
+        return ref[window, :].astype(jnp.float32), level
+
+    pairs = list(zip(share(mine_ref), share(other_ref)))
+    first = [jnp.where(first_here, mine, other) for mine, other in pairs]
+    second = [jnp.where(first_here, other, mine) for mine, other in pairs]
+    return blend(first, second, diagonal)
+
+
+def store_shares(shares, out_ref):
+    rows = shares[0][0].shape[0]
+    for request, (mean, _) in enumerate(shares):
+        out_ref[pl.ds(request * rows, rows), :] = mean.astype(jnp.bfloat16)
+    tail = tail_rows([level for _, level in shares])
+    out_ref[pl.ds(len(shares) * rows, tail.shape[0]), :] = tail
 
 
 def merge_kernel(bit, requests, mine_ref, other_ref, out_ref):
     rows = mine_ref.shape[1]
     diagonal = unit(rows)
-    levels = []
-    for request in range(requests):
-        mean, level = merged(bit, mine_ref, other_ref, request, requests, rows, diagonal)
-        out_ref[pl.ds(request * rows, rows), :] = mean.astype(jnp.bfloat16)
-        levels.append(level)
-    tail = tail_rows(levels)
-    out_ref[pl.ds(requests * rows, tail.shape[0]), :] = tail
+    shares = [
+        merged(bit, mine_ref, other_ref, request, requests, rows, diagonal)
+        for request in range(requests)
+    ]
+    store_shares(shares, out_ref)
+
+
+def first_merge_kernel(
+    scale, join_ref, q_ref, fresh_ref, mine_ref, other_ref, out_ref, score_ref
+):
+    steps, requests, group, depth = q_ref.shape
+    rows = steps * group
+    resident = requests - 1
+    diagonal = unit(rows)
+    shares = [
+        merged(1, mine_ref, other_ref, request, requests, rows, diagonal)
+        for request in range(requests)
+    ]
+    joined = join_ref[0]
+    owner = lax.axis_index("seq") < 2
+    recent = fresh_bias(steps, group, resident, resident, joined, owner)
+    parts = [(fresh_ref.at[0, resident], fresh_ref.at[1, resident], recent)]
+    state = attend(query_rows(q_ref, resident), parts, scale, score_ref)
+    mean, level = blend(shares[resident], finish(state, diagonal), diagonal)
+    step = lax.broadcasted_iota(jnp.int32, (rows, depth), 0) // group
+    shares[resident] = jnp.where(step >= joined, mean, 0.0), level
+    store_shares(shares, out_ref)
 
 
 def final_kernel(bit, mine_ref, other_ref, out_ref):
@@ -251,7 +332,7 @@
     return math.prod(array.shape) * jnp.dtype(array.dtype).itemsize
 
 
-def call(kernel, out_shape, in_specs, out_specs, flops, scratch=()):
+def call(kernel, out_shape, in_specs, out_specs, flops, scratch=(), grant=0):
     def run(*operands):
         blocks = [
             array
@@ -270,7 +351,7 @@
             cost_estimate=pl.CostEstimate(
                 flops=flops, bytes_accessed=held, transcendentals=0
             ),
-            compiler_params=pltpu.CompilerParams(vmem_limit_bytes=held + (2 << 20)),
+            compiler_params=pltpu.CompilerParams(vmem_limit_bytes=max(held + (2 << 20), grant)),
         )(*operands)
 
     return run
@@ -284,16 +365,23 @@
     ]
 
 
-def head_exchange(prefill, head_index, head_count):
-    held = [prefill]
+def head_exchange(far, send_near, near, head_index, head_count):
+    def pairs(bit):
+        return [(index, index ^ bit) for index in range(head_count)]
+
     bit = head_count // 2
+    arrived = lax.ppermute(far, "head", pairs(bit))
+    bit //= 2
+    held = [near, lax.ppermute(send_near, "head", pairs(bit))]
+    mine, other = halves(arrived, head_index)
+    held += [mine, lax.ppermute(other, "head", pairs(bit))]
+    bit //= 2
     while bit:
-        pairs = [(index, index ^ bit) for index in range(head_count)]
         split_up = [halves(part, head_index) for part in held]
-        sent = [lax.ppermute(other, "head", pairs) for _, other in split_up]
+        sent = [lax.ppermute(other, "head", pairs(bit)) for _, other in split_up]
         held = [mine for mine, _ in split_up] + sent
         bit //= 2
-    return held[1:]
+    return held
 
 
 def per_device(queries, new_kv, res_kv, prefill_kv, block_table, lengths, join_step):
@@ -309,20 +397,34 @@
     dev_blocks = total_blocks // senders
     block_len = new_rows // dev_blocks
     slots = total_blocks // seq_count
-    assert dev_blocks == seq_count and head_total == head_count and rows == depth
-    assert seq_count & (seq_count - 1) == 0 and head_count & (head_count - 1) == 0
+    assert head_count % 4 == 0 and dev_blocks == seq_count and head_total == head_count and rows == depth
+    assert seq_count >= 4 and seq_count & (seq_count - 1) == 0 and head_count & (head_count - 1) == 0
     scale = LOG2E / math.sqrt(depth)
     bf16, f32 = jnp.bfloat16, jnp.float32
     blocks = prefill_kv.reshape(2, head_total, dev_blocks, block_len, depth)
     fresh = jnp.transpose(new_kv[:, :, :, 0], (0, 2, 1, 3))
-    sources = head_exchange(prefill_kv, lax.axis_index("head"), head_count)
-    outgoing = call(
+
+    def heads_of(count):
+        return jax.ShapeDtypeStruct((2, count, dev_blocks, block_len, depth), bf16)
+
+    outgoing, far, send_near, near = call(
         functools.partial(pack_kernel, slots),
-        jax.ShapeDtypeStruct((senders, 2, block_len, depth), bf16),
-        [smem(), vmem()],
-        vmem(),
+        (
+            jax.ShapeDtypeStruct((senders, 2, block_len, depth), bf16),
+            heads_of(head_count // 2),
+            heads_of(head_count // 4),
+            heads_of(head_count // 4),
+        ),
+        [hbm()] * 2,
+        [vmem()] * 4,
         PACK_FLOPS,
-    )(block_table, blocks)
+        [
+            pltpu.SMEM((total_blocks,), jnp.int32),
+            pltpu.SemaphoreType.DMA((4 + 2 * dev_blocks,)),
+        ],
+    )(in_hbm(block_table), in_hbm(blocks))
+    sources = head_exchange(far, send_near, near, lax.axis_index("head"), head_count)
+    sources = [part.reshape(2, 1, new_rows, depth) for part in sources]
     arrived = lax.all_to_all(
         outgoing, ("seq", "head"), split_axis=0, concat_axis=0, tiled=True
     )
@@ -334,30 +436,40 @@
             jax.ShapeDtypeStruct((resident * rows, depth), bf16),
             jax.ShapeDtypeStruct((resident, rows), f32),
         ),
-        [smem(), vmem(), vmem(), vmem()],
+        [vmem()] * 3 + [hbm()],
         (vmem(), vmem()),
         4 * resident * rows * res_rows * depth,
         [
+            pltpu.VMEM((2, resident, res_rows, depth), bf16),
             pltpu.VMEM((resident, rows, padded), f32),
+            pltpu.SemaphoreType.DMA((2, resident)),
         ],
-    )(lengths, queries, fresh, res_kv[:, :, :, 0])
-
-    padded = head_count * new_rows + -(-steps // 128) * 128
+    )(lengths.reshape(1, requests), queries, fresh, in_hbm(res_kv[:, :, :, 0]))
+
     payload = call(
         functools.partial(joining_kernel, scale, len(sources)),
         jax.ShapeDtypeStruct((requests * rows + 16 * -(-requests * PIECES // 16), depth), bf16),
-        [smem()] + [vmem()] * (5 + len(sources)),
+        [vmem()] * (3 + len(sources)),
         vmem(),
         4 * rows * head_count * new_rows * depth,
-        [pltpu.VMEM((rows, padded), f32)],
-    )(join_step, queries, fresh, res_mean, res_level, prefill_kv, *sources)
+        [pltpu.VMEM((rows, head_count * new_rows), f32)],
+    )(queries, res_mean, res_level, *sources)
 
     bit = 1
     while bit < seq_count:
         pairs = [(index, index ^ bit) for index in range(seq_count)]
         last = 2 * bit >= seq_count
         other = lax.ppermute(payload, "seq", pairs)
-        if not last:
+        if bit == 1:
+            payload = call(
+                functools.partial(first_merge_kernel, scale),
+                jax.ShapeDtypeStruct(payload.shape, bf16),
+                [smem()] + [vmem()] * 4,
+                vmem(),
+                1 << 20,
+                [pltpu.VMEM((rows, 128), f32)],
+            )(join_step, queries, fresh, payload, other)
+        elif not last:
             payload = call(
                 functools.partial(merge_kernel, bit, requests),
                 jax.ShapeDtypeStruct(payload.shape, bf16),

time: 47.5 us -> 44.9 us (0.945)
  local copies, waits for them, and re-layouts: 3.94 us -> 0.04 us
  Pallas kernels: 7.4 us -> 9.56 us
  waiting for transfers between devices: 20 us -> 19.4 us
    unnamed x16 -> x8, local copies, waits for them, and re-layouts: 3.89 us -> 0.02 us
    pallas_call x6, Pallas kernels: 7.4 us -> 9.56 us  [run(): pl.pallas_call(kernel, out_shape=out_shape, in_specs=in_specs, out_specs=...]
    ppermute x2, waiting for transfers between devices: 8.59 us -> 7.87 us  [per_device(): other = lax.ppermute(payload, 'seq', pairs)]
  transfers between devices with their start and end apart: 6 -> 6, of which waited for: 3 -> 3; matrix products, arithmetic and copies ran while one was open for 0% -> 0% of each run, Pallas kernels for 9% -> 12%
where the time goes in v4:
time: 44.9 us; the launch traced here: 44.6 us
  waiting for transfers between devices  19.4 us (43%)
  starting transfers between devices  14.2 us (32%)
  Pallas kernels  9.56 us (21%)
  between operations  1.41 us (3%)
    ppermute x1, waiting for transfers between devices, head_exchange(): arrived = lax.ppermute(far, 'head', pairs(bit))  11.6 us
    pallas_call x6, Pallas kernels, run(): pl.pallas_call(kernel, out_shape=out_shape, in_specs=in_specs, out_specs=...  9.56 us
    ppermute x2, waiting for transfers between devices, per_device(): other = lax.ppermute(payload, 'seq', pairs)  7.87 us
    all_to_all x1, starting transfers between devices, per_device(): lax.all_to_all(outgoing, ('seq', 'head'), split_axis=0, concat_axis=0, ti...  7.4 us
    ppermute x2, starting transfers between devices, per_device(): other = lax.ppermute(payload, 'seq', pairs)  4.8 us
    ppermute x1, starting transfers between devices, head_exchange(): arrived = lax.ppermute(far, 'head', pairs(bit))  1.93 us
  transfers between devices with their start and end apart: 6, of which 3 were waited for; matrix products, arithmetic and copies ran while one was open for 0% of the time, Pallas kernels for 12%

profile of v4, /device:TPU:0, one launch (start us, length us, event | category | flops | bytes accessed | tf_op | source)
XLA Modules:
  0.0 44.6 jit_solution(8248482978480247292)
XLA Ops:
  0.6 0.0 copy-start
  0.6 0.0 copy-start.1
  0.7 0.0 copy-start.2
  0.7 2.7 %shard_map.87 = (bf16[16,2,64,128]{3,2,1,0:T(8,128)(2,1)}, bf16[2,2,4,64,128]{4,3,2,1,0:T(8,128)(2,1)S(1)}, bf16[2,1,4,64,128]{4,3,2,1,0:T(8,128)(2,1)S(1)}, bf16[2,1,4,64,128]{4,3,2,1,0:T(8,128)(2,1)S(1)}) custom-call(s32[64]{0:T(128)} %table_ref.1, bf16[2,4,4,64,128]{4,3,2,1,0:T(8,128)(2,1)} %bitcast.22), custom_call_target="tpu_custom_call" | custom-call | flops 8589934592 | bytes 1048576 | tf_op jit(solution)/shard_map/pallas_call | solution.py:345
  3.4 0.0 copy-start.3
  3.4 7.4 %all-to-all-start = ((bf16[16,2,64,128]{3,2,1,0:T(8,128)(2,1)}), bf16[16,2,64,128]{3,2,1,0:T(8,128)(2,1)S(1)}, u32[]{:S(2)}, u32[]{:S(2)}) async-start(bf16[16,2,64,128]{3,2,1,0:T(8,128)(2,1)} %get-tuple-element.13), calls=%async_computation | async-start | bytes 1048576 | tf_op jit(solution)/shard_map/all_to_all | solution.py:428
  10.8 1.9 %collective-permute-start.1 = (bf16[2,2,4,64,128]{4,3,2,1,0:T(8,128)(2,1)S(1)}, bf16[2,2,4,64,128]{4,3,2,1,0:T(8,128)(2,1)S(1)}, u32[]{:S(2)}, u32[]{:S(2)}) collective-permute-start(bf16[2,2,4,64,128]{4,3,2,1,0:T(8,128)(2,1)S(1)} %get-tuple-element.12), channel_id=1, source_target_pairs={{0,2},{1,3},{2,0},{3,1},{4,6},{5,7},{6,4},{7,5},{8,10},{9,11},{10,... | collective-permute-start | bytes 786440 | tf_op jit(solution)/shard_map/ppermute | solution.py:373
  12.7 0.0 collective-permute-start
  12.8 11.6 %collective-permute-done.1 = bf16[2,2,4,64,128]{4,3,2,1,0:T(8,128)(2,1)S(1)} collective-permute-done((bf16[2,2,4,64,128]{4,3,2,1,0:T(8,128)(2,1)S(1)}, bf16[2,2,4,64,128]{4,3,2,1,0:T(8,128)(2,1)S(1)}, u32[]{:S(2)}, u32[]{:S(2)}) %collective-permute-start.1) | collective-permute-done | bytes 262176 | tf_op jit(solution)/shard_map/ppermute | solution.py:373
  24.3 0.1 collective-permute-start.2
  24.4 0.0 copy-done
  24.4 0.0 copy-done.1
  24.4 0.0 copy-done.2
  24.4 3.4 %shard_map.86 = (bf16[256,128]{1,0:T(8,128)(2,1)S(1)}, f32[2,128]{1,0:T(2,128)S(1)}) custom-call(s32[1,3]{1,0:T(1,128)S(1)} %bitcast.19, bf16[16,3,8,128]{3,2,1,0:T(8,128)(2,1)S(1)} %copy-done, bf16[2,3,16,128]{3,2,1,0:T(8,128)(2,1)S(1)} %bitcast.17, bf16[2,2,4096,128]{3,2,1,0:T(8,128)(2,1)} %bitcast.20), custom_call_target="tpu_custom_call" | custom-call | flops 536870912 | bytes 8709132 | tf_op jit(solution)/shard_map/pallas_call | solution.py:345
  27.9 0.0 collective-permute-done
  27.9 0.0 collective-permute-done.2
  27.9 0.5 %shard_map.88.mine_ref = bf16[400,128]{1,0:T(8,128)(2,1)S(1)} custom-call(bf16[16,3,8,128]{3,2,1,0:T(8,128)(2,1)S(1)} %copy-done, bf16[256,128]{1,0:T(8,128)(2,1)S(1)} %get-tuple-element.8.res_ref, f32[2,128]{1,0:T(2,128)S(1)} %get-tuple-element.9.res_level_ref, bf16[2,1,256,128]{3,2,1,0:T(8,128)(2,1)S(1)} %bitcast.14, ...), custom_call_target="tpu_custom_call" | custom-call | flops 67108864 | bytes 1315840 | tf_op jit(solution)/shard_map/pallas_call | solution.py:345
  28.4 2.0 %collective-permute-start.3 = (bf16[400,128]{1,0:T(8,128)(2,1)S(1)}, bf16[400,128]{1,0:T(8,128)(2,1)S(1)}, u32[]{:S(2)}, u32[]{:S(2)}) collective-permute-start(bf16[400,128]{1,0:T(8,128)(2,1)S(1)} %shard_map.88.mine_ref), channel_id=1, source_target_pairs={{0,4},{4,0},{8,12},{12,8},{1,5},{5,1},{9,13},{13,9},{2,6},{6,2},{1... | collective-permute-start | bytes 307208 | tf_op jit(solution)/shard_map/ppermute | solution.py:462
  31.1 2.9 %collective-permute-done.3.other_ref = bf16[400,128]{1,0:T(8,128)(2,1)S(1)} collective-permute-done((bf16[400,128]{1,0:T(8,128)(2,1)S(1)}, bf16[400,128]{1,0:T(8,128)(2,1)S(1)}, u32[]{:S(2)}, u32[]{:S(2)}) %collective-permute-start.3) | collective-permute-done | bytes 102432 | tf_op jit(solution)/shard_map/ppermute | solution.py:462
  34.0 0.4 %shard_map.89.mine_ref = bf16[400,128]{1,0:T(8,128)(2,1)S(1)} custom-call(s32[1]{0:T(128)S(6)} %copy.10.join_ref, bf16[16,3,8,128]{3,2,1,0:T(8,128)(2,1)S(1)} %copy-done, bf16[2,3,16,128]{3,2,1,0:T(8,128)(2,1)S(1)} %bitcast.18, bf16[400,128]{1,0:T(8,128)(2,1)S(1)} %shard_map.88.mine_ref, bf16[400,128]{1,0:T(8,128)(2,1)S(1)} %collective-permute-done.3.other_ref), custom_call_target="tpu_custom_call" | custom-call | flops 1048576 | bytes 495616 | tf_op jit(solution)/shard_map/pallas_call | solution.py:345
  34.4 2.8 %collective-permute-start.4 = (bf16[400,128]{1,0:T(8,128)(2,1)S(1)}, bf16[400,128]{1,0:T(8,128)(2,1)S(1)}, u32[]{:S(2)}, u32[]{:S(2)}) collective-permute-start(bf16[400,128]{1,0:T(8,128)(2,1)S(1)} %shard_map.89.mine_ref), channel_id=1, source_target_pairs={{0,8},{4,12},{8,0},{12,4},{1,9},{5,13},{9,1},{13,5},{2,10},{6,14},... | collective-permute-start | bytes 307208 | tf_op jit(solution)/shard_map/ppermute | solution.py:462
  37.2 5.0 %collective-permute-done.4.other_ref = bf16[400,128]{1,0:T(8,128)(2,1)S(1)} collective-permute-done((bf16[400,128]{1,0:T(8,128)(2,1)S(1)}, bf16[400,128]{1,0:T(8,128)(2,1)S(1)}, u32[]{:S(2)}, u32[]{:S(2)}) %collective-permute-start.4) | collective-permute-done | bytes 102432 | tf_op jit(solution)/shard_map/ppermute | solution.py:462
  42.2 0.8 %shard_map.90 = bf16[16,3,8,128]{3,2,1,0:T(8,128)(2,1)} custom-call(bf16[400,128]{1,0:T(8,128)(2,1)S(1)} %shard_map.89.mine_ref, bf16[400,128]{1,0:T(8,128)(2,1)S(1)} %collective-permute-done.4.other_ref), custom_call_target="tpu_custom_call" | custom-call | flops 1048576 | bytes 303104 | tf_op jit(solution)/shard_map/pallas_call | solution.py:345
  43.1 0.0 all-to-all-done.arrived_ref
  43.1 0.0 copy-done.3
  43.1 1.6 %shard_map.91 = bf16[2,16,64,128]{3,2,1,0:T(8,128)(2,1)} custom-call(s32[64]{0:T(128)S(1)} %copy-done.3, bf16[16,2,64,128]{3,2,1,0:T(8,128)(2,1)S(1)} %all-to-all-done.arrived_ref), custom_call_target="tpu_custom_call" | custom-call | flops 1048576 | bytes 1048576 | tf_op jit(solution)/shard_map/pallas_call | solution.py:345
  (1 shorter events, 0.0 us)
Async XLA Ops:
  0.6 23.8 %copy-start = (bf16[16,3,8,128]{3,2,1,0:T(8,128)(2,1)S(1)}, bf16[16,3,8,128]{3,2,1,0:T(8,128)(2,1)}, u32[]{:S(2)}) copy-start(bf16[16,3,8,128]{3,2,1,0:T(8,128)(2,1)} %q_ref.5) | copy-start | bytes 294916
  0.6 23.8 %copy-start.1 = (bf16[2,16,3,1,128]{4,1,3,2,0:T(8,128)(2,1)S(1)}, bf16[2,16,3,1,128]{4,1,3,2,0:T(8,128)(2,1)}, u32[]{:S(2)}) copy-start(bf16[2,16,3,1,128]{4,1,3,2,0:T(8,128)(2,1)} %param.8) | copy-start | bytes 73732
  0.7 23.8 %copy-start.2 = (s32[3]{0:T(128)S(1)}, s32[3]{0:T(128)}, u32[]{:S(2)}) copy-start(s32[3]{0:T(128)} %param.12) | copy-start | bytes 40
  3.4 39.7 %copy-start.3 = (s32[64]{0:T(128)S(1)}, s32[64]{0:T(128)}, u32[]{:S(2)}) copy-start(s32[64]{0:T(128)} %table_ref.1) | copy-start | bytes 772
  3.4 39.7 %all-to-all-start = ((bf16[16,2,64,128]{3,2,1,0:T(8,128)(2,1)}), bf16[16,2,64,128]{3,2,1,0:T(8,128)(2,1)S(1)}, u32[]{:S(2)}, u32[]{:S(2)}) async-start(bf16[16,2,64,128]{3,2,1,0:T(8,128)(2,1)} %get-tuple-element.13), calls=%async_computation | async-start | bytes 1048576 | tf_op jit(solution)/shard_map/all_to_all | solution.py:428
  10.8 13.5 %collective-permute-start.1 = (bf16[2,2,4,64,128]{4,3,2,1,0:T(8,128)(2,1)S(1)}, bf16[2,2,4,64,128]{4,3,2,1,0:T(8,128)(2,1)S(1)}, u32[]{:S(2)}, u32[]{:S(2)}) collective-permute-start(bf16[2,2,4,64,128]{4,3,2,1,0:T(8,128)(2,1)S(1)} %get-tuple-element.12), channel_id=1, source_target_pairs={{0,2},{1,3},{2,0},{3,1},{4,6},{5,7},{6,4},{7,5},{8,10},{9,11},{10,... | collective-permute-start | bytes 786440 | tf_op jit(solution)/shard_map/ppermute | solution.py:373
  12.7 15.1 %collective-permute-start = (bf16[2,1,4,64,128]{4,3,2,1,0:T(8,128)(2,1)S(1)}, bf16[2,1,4,64,128]{4,3,2,1,0:T(8,128)(2,1)S(1)}, u32[]{:S(2)}, u32[]{:S(2)}) collective-permute-start(bf16[2,1,4,64,128]{4,3,2,1,0:T(8,128)(2,1)S(1)} %get-tuple-element.11), channel_id=1, source_target_pairs={{0,1},{1,0},{2,3},{3,2},{4,5},{5,4},{6,7},{7,6},{8,9},{9,8},{10,11... | collective-permute-start | bytes 393224 | tf_op jit(solution)/shard_map/ppermute | solution.py:375
  24.3 3.6 %collective-permute-start.2 = (bf16[2,1,4,64,128]{4,3,2,1,0:T(8,128)(2,1)S(1)}, bf16[2,1,4,64,128]{4,3,2,1,0:T(8,128)(2,1)S(1)}, u32[]{:S(2)}, u32[]{:S(2)}) collective-permute-start(bf16[2,1,4,64,128]{4,3,2,1,0:T(8,128)(2,1)S(1)} %get-tuple-element.16), channel_id=1, source_target_pairs={{0,1},{1,0},{2,3},{3,2},{4,5},{5,4},{6,7},{7,6},{8,9},{9,8},{10,11... | collective-permute-start | bytes 393224 | tf_op jit(solution)/shard_map/ppermute | solution.py:377
  28.4 5.5 %collective-permute-start.3 = (bf16[400,128]{1,0:T(8,128)(2,1)S(1)}, bf16[400,128]{1,0:T(8,128)(2,1)S(1)}, u32[]{:S(2)}, u32[]{:S(2)}) collective-permute-start(bf16[400,128]{1,0:T(8,128)(2,1)S(1)} %shard_map.88.mine_ref), channel_id=1, source_target_pairs={{0,4},{4,0},{8,12},{12,8},{1,5},{5,1},{9,13},{13,9},{2,6},{6,2},{1... | collective-permute-start | bytes 307208 | tf_op jit(solution)/shard_map/ppermute | solution.py:462
  34.4 7.8 %collective-permute-start.4 = (bf16[400,128]{1,0:T(8,128)(2,1)S(1)}, bf16[400,128]{1,0:T(8,128)(2,1)S(1)}, u32[]{:S(2)}, u32[]{:S(2)}) collective-permute-start(bf16[400,128]{1,0:T(8,128)(2,1)S(1)} %shard_map.89.mine_ref), channel_id=1, source_target_pairs={{0,8},{4,12},{8,0},{12,4},{1,9},{5,13},{9,1},{13,5},{2,10},{6,14},... | collective-permute-start | bytes 307208 | tf_op jit(solution)/shard_map/ppermute | solution.py:462
